TPU v7x, 128 devices: a whole 4x4x4 slice. The times are simulated.
128 devices in a mesh: rows: 2 (over core), cols: 64 (over z, y, x).
Axes of the slice: x: 4, y: 4, z: 4, core: 2. Of those that a mesh axis runs over, the one named last changes fastest.
Arguments:
- jacobian: float32 [32768, 16384], P('rows', 'cols'), may hold values from -0.046875 to 0.046875
- targets: float32 [64, 32768], P(None, 'rows'), may hold values from 0 to 1
- anchor: float32 [64, 16384], P(None, 'cols'), may hold values from -6 to 6
- precision: float32 [16384], P('cols'), may hold values from 0.3 to 3
Outputs:
- samples: float32 [64, 16384], P(None, 'cols')
All inputs are finite; a program needn't handle non-finite values.
Results may differ from a plain program's by a relative error of at most 0.0001.
Values sent between devices are 32-bit elements; how exact they have to be, the bound alone decides.
No kernel may reach another device: no remote copies, remote signals or barrier semaphores. Data moves between devices by JAX's collectives and lax.ppermute only.
A program may use at most 128 MiB of HBM per device.

v0:
```python
import math

import jax
import jax.numpy as jnp
from jax import lax
from jax.experimental import pallas as pl
from jax.experimental.pallas import tpu as pltpu
from jax.sharding import Mesh
from jax.sharding import PartitionSpec as P

STEPS = 3
SIDE = 4
CUBE = 8
SHIFT = (0, 1, 1)
AXES = ("rows", "z", "y", "x")
COLS = ("z", "y", "x")
LANES = 128
TAIL = 8
F32 = jnp.float32
BF16 = jnp.bfloat16
ACROSS = (((1,), (1,)), ((), ()))
DOWN = (((1,), (0,)), ((), ()))
WHOLE = pl.BlockSpec(memory_space=pltpu.VMEM)


def place(core, at):
    turned = [(p + core + s) & (SIDE - 1) for p, s in zip(at, SHIFT)]
    half = [((t + 1) >> 1) & 1 for t in turned]
    pair = [t >> 1 for t in turned]
    return half[0] * 4 + half[1] * 2 + half[2], pair[0] * 4 + pair[1] * 2 + pair[2]


def cube_groups():
    first, second = {}, {}
    for device in range(2 * SIDE**3):
        core, z, y, x = device // 64, device // 16 % 4, device // 4 % 4, device % 4
        half, pair = place(core, (z, y, x))
        first.setdefault((core, pair), {})[half] = device
        second.setdefault((core, half), {})[pair] = device
    in_order = lambda groups: [[group[k] for k in range(CUBE)] for _, group in sorted(groups.items())]
    return in_order(first), in_order(second)


FIRST, SECOND = cube_groups()


def exchange(x, groups):
    return lax.all_to_all(x, AXES, split_axis=0, concat_axis=0, axis_index_groups=groups, tiled=True)


def own_block():
    return place(lax.axis_index("rows"), [lax.axis_index(a) for a in COLS])


def call(kernel, out_shape, name, mib, **kw):
    return pl.pallas_call(
        kernel,
        out_shape=out_shape,
        name=name,
        compiler_params=pltpu.CompilerParams(vmem_limit_bytes=mib << 20),
        **kw,
    )


def array(*shape, dtype=F32):
    return jax.ShapeDtypeStruct(shape, dtype)


def halves(x):
    high = x.astype(BF16)
    return high, (x - high.astype(F32)).astype(BF16)


def dot(a, b, dims):
    return lax.dot_general(a, b, dims, preferred_element_type=F32)


def diagonal(samples):
    shape = (samples, LANES)
    return lax.broadcasted_iota(jnp.int32, shape, 0) == lax.broadcasted_iota(jnp.int32, shape, 1)


def to_lanes(column):
    samples = column.shape[0]
    row = jnp.sum(jnp.where(diagonal(samples), column, 0.0), axis=0, keepdims=True)
    return jnp.broadcast_to(row, (TAIL, LANES))


def to_column(row, samples):
    return jnp.sum(jnp.where(diagonal(samples), row, 0.0), axis=1, keepdims=True)


def stacked(x):
    high, low = halves(x)
    return jnp.concatenate([high, low], 0), high


def put_part(out_ref, j, both, high, flip_high, flip_low, tail):
    samples = high.shape[0]
    tiles = flip_high.shape[1] // LANES
    wide = dot(both, flip_high, DOWN)
    logits = wide[:samples] + wide[samples:] + dot(high, flip_low, DOWN)
    for t in range(tiles):
        out_ref[j, t * samples : (t + 1) * samples] = logits[:, t * LANES : (t + 1) * LANES]
    out_ref[j, tiles * samples :] = tail


def open_kernel(at_ref, targets_ref, theta_ref, jac_ref, out_ref, own_ref, *refs):
    high_ref, low_ref, flip_high_ref, flip_low_ref, both_ref = refs
    samples, cols = theta_ref.shape[1:]
    j = pl.program_id(0)
    part = jac_ref.shape[1]

    @pl.when(j == 0)
    def _():
        for t in range(targets_ref.shape[1] // LANES):
            own_ref[t * samples : (t + 1) * samples] = targets_ref[:, t * LANES : (t + 1) * LANES]
        for c in range(CUBE):
            both_ref[:, c * cols : (c + 1) * cols], _ = stacked(theta_ref[c])

    rows = pl.ds(pl.multiple_of(j * part, part), part)
    for c in range(CUBE):
        jac_high, jac_low = halves(jac_ref[c])
        at = slice(c * cols, (c + 1) * cols)
        high_ref[rows, at] = jac_high
        low_ref[rows, at] = jac_low
        flip_high_ref[j, at] = jnp.transpose(jac_high)
        flip_low_ref[j, at] = jnp.transpose(jac_low)
    both = both_ref[...]
    put_part(out_ref, 0, both, both[:samples], flip_high_ref[j], flip_low_ref[j], jnp.zeros((TAIL, LANES), F32))


def opened(at, targets, theta, jacobian):
    samples, cols = theta.shape[1:]
    rows = jacobian.shape[1]
    part = rows // CUBE
    length = part // LANES * samples
    return pl.pallas_call(
        open_kernel,
        name="opened",
        out_shape=[
            array(CUBE, length + TAIL, LANES),
            array(length, LANES),
            array(rows, CUBE * cols, dtype=BF16),
            array(rows, CUBE * cols, dtype=BF16),
            array(CUBE, CUBE * cols, part, dtype=BF16),
            array(CUBE, CUBE * cols, part, dtype=BF16),
        ],
        grid_spec=pltpu.PrefetchScalarGridSpec(
            num_scalar_prefetch=1,
            grid=(CUBE,),
            in_specs=[
                pl.BlockSpec((samples, part), lambda j, at: (0, at[0])),
                WHOLE,
                pl.BlockSpec((CUBE, part, cols), lambda j, at: (0, j, 0)),
            ],
            out_specs=[pl.BlockSpec((1, length + TAIL, LANES), lambda j, at: (j, 0, 0))] + [WHOLE] * 5,
            scratch_shapes=[pltpu.VMEM((2 * samples, CUBE * cols), BF16)],
        ),
        compiler_params=pltpu.CompilerParams(vmem_limit_bytes=12 << 20),
    )(at, in_hbm(targets), theta, in_hbm(jacobian))


def in_hbm(x):
    return pltpu.with_memory_space_constraint(x, pltpu.HBM)


def fold_kernel(in_ref, out_ref):
    out_ref[...] = jnp.sum(in_ref[...], axis=0)


def fold(parts):
    return call(fold_kernel, array(*parts.shape[1:]), "fold", 4, in_specs=[WHOLE], out_specs=WHOLE)(parts)


def scale_from(row, samples, clip_level, params):
    squares = to_column(row, samples)
    return jnp.minimum(1.0, clip_level / jnp.sqrt(squares / params + 1e-06))


def residual_to(out_ref, logits, targets):
    residual = jax.nn.sigmoid(logits) - targets
    for i in range(CUBE):
        out_ref[i] = residual


def first_residual_kernel(in_ref, targets_ref, residual_ref, logits_ref):
    logits = jnp.sum(in_ref[:, : targets_ref.shape[0]], axis=0)
    logits_ref[...] = logits
    residual_to(residual_ref, logits, targets_ref[...])


def first_residual(parts, targets):
    return call(
        first_residual_kernel,
        [array(CUBE, *targets.shape), array(*targets.shape)],
        "first_residual",
        4,
        in_specs=[WHOLE] * 2,
        out_specs=[WHOLE] * 2,
    )(parts, targets)


def next_residual(parts, targets, logits, slope, samples, clip_level, params):
    def kernel(in_ref, targets_ref, logits_ref, slope_ref, residual_ref, out_logits_ref, out_slope_ref, scale_ref):
        length = targets_ref.shape[0]
        row = jnp.sum(in_ref[:, length:], axis=0)[:1]
        scale = scale_from(row, samples, clip_level, params)
        scale_ref[...] = jnp.broadcast_to(scale, scale_ref.shape)
        moved = jnp.sum(in_ref[:, :length], axis=0)
        for t in range(length // samples):
            at = slice(t * samples, (t + 1) * samples)
            out_slope_ref[at] = 0.9 * slope_ref[at] + scale * moved[at]
        logits = logits_ref[...] - 0.5 * out_slope_ref[...]
        out_logits_ref[...] = logits
        residual_to(residual_ref, logits, targets_ref[...])

    shape = targets.shape
    return call(
        kernel,
        [array(CUBE, *shape), array(*shape), array(*shape), array(samples, LANES)],
        "next_residual",
        4,
        in_specs=[WHOLE] * 4,
        out_specs=[WHOLE] * 4,
    )(parts, targets, logits, slope)


def joined(in_ref, samples):
    blocks, length = in_ref.shape[0], in_ref.shape[1] // samples * samples
    return jnp.concatenate([in_ref[b, t : t + samples] for b in range(blocks) for t in range(0, length, samples)], 1)


def gradient_kernel(residual_ref, high_ref, low_ref, out_ref):
    samples, cols = out_ref.shape[1:]
    both, high = stacked(joined(residual_ref, samples))
    for c in range(CUBE):
        at = slice(c * cols, (c + 1) * cols)
        wide = dot(both, high_ref[:, at], DOWN)
        out_ref[c] = wide[:samples] + wide[samples:] + dot(high, low_ref[:, at], DOWN)


def gradient_parts(residual, high, low, samples):
    return call(
        gradient_kernel,
        array(CUBE, samples, high.shape[1] // CUBE),
        "gradient",
        6,
        in_specs=[WHOLE] * 3,
        out_specs=WHOLE,
    )(residual, high, low)


def moved_on(state):
    theta_ref, velocity_ref, gradient_ref, scale_ref = state
    velocity = 0.9 * velocity_ref[...] + scale_ref[:, :1] * gradient_ref[...]
    return theta_ref[...] - 0.5 * velocity, velocity


def whole_gradient(own_ref, other_ref, prec_ref, anchor_ref, theta):
    gradient = own_ref[...] + other_ref[...] + prec_ref[...] * (theta - anchor_ref[...])
    return gradient, jnp.sum(gradient * gradient, axis=1, keepdims=True)


def send_gradient(out_ref, gradient, square):
    samples, cols = gradient.shape
    tail = to_lanes(square)
    for c in range(CUBE):
        for t in range(cols // LANES):
            out_ref[c, t * samples : (t + 1) * samples] = gradient[:, t * LANES : (t + 1) * LANES]
        out_ref[c, cols // LANES * samples :] = tail


def first_step_kernel(own_ref, other_ref, prec_ref, anchor_ref, out_ref, gradient_ref):
    gradient, square = whole_gradient(own_ref, other_ref, prec_ref, anchor_ref, anchor_ref[...])
    gradient_ref[...] = gradient
    send_gradient(out_ref, gradient, square)


def next_step_kernel(own_ref, other_ref, prec_ref, anchor_ref, *refs):
    state, (out_ref, gradient_ref, theta_ref, velocity_ref) = refs[:4], refs[4:]
    theta, velocity = moved_on(state)
    theta_ref[...] = theta
    velocity_ref[...] = velocity
    gradient, square = whole_gradient(own_ref, other_ref, prec_ref, anchor_ref, theta)
    gradient_ref[...] = gradient
    send_gradient(out_ref, gradient, square)


def stepped(own, other, prec, anchor, state=()):
    samples, cols = anchor.shape
    outs = 3 if state else 1
    return call(
        next_step_kernel if state else first_step_kernel,
        [array(CUBE, cols // LANES * samples + TAIL, LANES)] + [array(samples, cols)] * outs,
        "next_step" if state else "first_step",
        4,
        in_specs=[WHOLE] * (4 + len(state)),
        out_specs=[WHOLE] * (1 + outs),
    )(own, other, prec, anchor, *state)


def push(parts, flip_high, flip_low, samples):
    def kernel(in_ref, high_ref, low_ref, out_ref):
        both, first = stacked(joined(in_ref, samples))
        tail = jnp.sum(in_ref[:, -TAIL:], axis=0)
        for j in range(CUBE):
            put_part(out_ref, j, both, first, high_ref[j], low_ref[j], tail)

    return call(
        kernel,
        array(CUBE, flip_high.shape[2] // LANES * samples + TAIL, LANES),
        "push",
        6,
        in_specs=[WHOLE] * 3,
        out_specs=WHOLE,
    )(parts, flip_high, flip_low)


def last_kernel(own_ref, other_ref, prec_ref, anchor_ref, *refs):
    state, (squares_ref, gradient_ref, theta_ref, velocity_ref) = refs[:4], refs[4:]
    theta, velocity = moved_on(state)
    theta_ref[...] = theta
    velocity_ref[...] = velocity
    gradient, square = whole_gradient(own_ref, other_ref, prec_ref, anchor_ref, theta)
    gradient_ref[...] = gradient
    squares_ref[...] = jnp.broadcast_to(to_lanes(square)[:1], squares_ref.shape)


def last_gradient(own, other, prec, anchor, state):
    shape = anchor.shape
    return call(
        last_kernel,
        [array(SIDE**3, LANES)] + [array(*shape)] * 3,
        "last_gradient",
        4,
        in_specs=[WHOLE] * 8,
        out_specs=[WHOLE] * 4,
    )(own, other, prec, anchor, *state)


def close(squares, theta, velocity, gradient, clip_level, params):
    samples = theta.shape[0]

    def kernel(squares_ref, theta_ref, velocity_ref, gradient_ref, out_ref):
        row = jnp.sum(squares_ref[...], axis=0, keepdims=True)
        scale = scale_from(row, samples, clip_level, params)
        velocity = 0.9 * velocity_ref[...] + scale * gradient_ref[...]
        out_ref[...] = theta_ref[...] - 0.5 * velocity

    return call(kernel, array(*theta.shape), "close", 4, in_specs=[WHOLE] * 4, out_specs=WHOLE)(
        squares, theta, velocity, gradient
    )


def body(jacobian, targets, anchor, precision):
    samples, col_dev = anchor.shape
    row_dev = jacobian.shape[0]
    params = col_dev * SIDE**3
    clip_level = 0.2 * math.sqrt(row_dev * 2 / params)
    half, pair = own_block()
    at = jnp.reshape(pair * CUBE + half, (1,)).astype(jnp.int32)
    prec = precision[None, :]
    jacobian, at = lax.optimization_barrier((jacobian, at))
    square = exchange(jacobian.reshape(CUBE, row_dev // CUBE, col_dev), SECOND)
    square, theta = lax.optimization_barrier((square, anchor))
    theta = exchange(jnp.broadcast_to(theta[None], (CUBE, samples, col_dev)), SECOND)
    parts, own, high, low, *flips = opened(at, targets, theta, square)
    residual, logits = first_residual(exchange(parts, FIRST), own)
    slope = jnp.zeros_like(logits)
    state = ()
    for step in range(STEPS):
        parts = gradient_parts(exchange(residual, FIRST), high, low, samples)
        gradient = fold(exchange(parts, SECOND))
        other = lax.ppermute(gradient, "rows", [(0, 1), (1, 0)])
        if step + 1 == STEPS:
            break
        parts, gradient, *moved = stepped(gradient, other, prec, anchor, state)
        theta, velocity = moved if moved else (anchor, jnp.zeros_like(anchor))
        parts = exchange(push(exchange(parts, SECOND), *flips, samples), FIRST)
        residual, logits, slope, scale = next_residual(parts, own, logits, slope, samples, clip_level, params)
        state = (theta, velocity, gradient, scale)
    squares, gradient, theta, velocity = last_gradient(gradient, other, prec, anchor, state)
    squares = lax.all_to_all(squares, COLS, split_axis=0, concat_axis=0, tiled=True)
    return close(squares, theta, velocity, gradient, clip_level, params)


def solution(mesh):
    cubes = Mesh(mesh.devices.reshape(2, SIDE, SIDE, SIDE), AXES)
    in_specs = (P("rows", COLS), P(None, "rows"), P(None, COLS), P(COLS))
    out_specs = P(None, COLS)
    return jax.shard_map(body, mesh=cubes, in_specs=in_specs, out_specs=out_specs, check_vma=False)
```

profile of v0, /device:TPU:0, one launch (start us, length us, event | category | flops | bytes accessed | tf_op | source)
XLA Modules:
  0.0 305.0 jit_solution(17056535024833345746)
XLA Ops:
  0.0 0.0 copy-start
  0.0 105.4 %all_to_all.76.jac_ref = f32[8,2048,256]{2,1,0:T(8,128)} all-to-all(f32[8,2048,256]{2,1,0:T(8,128)} %bitcast.12), channel_id=1, replica_groups={{15,14,11,10,63,62,59,58},{12,13,8,9,60,61,56,57},{3,2,7,6,51,50,55,54}..., dimensions={0} | all-to-all | bytes 33554432 | tf_op jit(solution)/shard_map/all_to_all | solution.py:48
  105.4 0.0 copy-done
  105.4 12.0 %all_to_all.77.theta_ref = f32[8,64,256]{2,1,0:T(8,128)S(1)} all-to-all(f32[8,64,256]{2,1,0:T(8,128)S(1)} %broadcast_in_dim.15), channel_id=1, replica_groups={{15,14,11,10,63,62,59,58},{12,13,8,9,60,61,56,57},{3,2,7,6,51,50,55,54}..., dimensions={0} | all-to-all | bytes 1048576 | tf_op jit(solution)/shard_map/all_to_all | solution.py:48
  117.4 11.5 %opened.1 = (f32[8,136,128]{2,1,0:T(8,128)S(1)}, f32[128,128]{1,0:T(8,128)S(1)}, bf16[2048,2048]{1,0:T(8,128)(2,1)S(1)}, bf16[2048,2048]{1,0:T(8,128)(2,1)S(1)},...) custom-call(s32[1]{0:T(128)} %bitcast.at_ref, f32[64,16384]{1,0:T(8,128)} %targets_ref.1, ...), custom_call_target="tpu_custom_call" | custom-call | tf_op jit(solution)/shard_map/opened/pallas_call | solution.py:138
  128.9 12.8 %all_to_all.78.in_ref = f32[8,136,128]{2,1,0:T(8,128)S(1)} all-to-all(f32[8,136,128]{2,1,0:T(8,128)S(1)} %get-tuple-element.37), channel_id=1, replica_groups={{15,12,3,0,31,28,19,16},{14,13,2,1,30,29,18,17},{11,8,7,4,27,24,23,20},..., dimensions={0} | all-to-all | bytes 1114112 | tf_op jit(solution)/shard_map/all_to_all | solution.py:48
  141.8 0.1 first_residual.1
  141.8 13.2 %all_to_all.79.residual_ref = f32[8,128,128]{2,1,0:T(8,128)S(1)} all-to-all(f32[8,128,128]{2,1,0:T(8,128)S(1)} %get-tuple-element.39), channel_id=1, replica_groups={{15,12,3,0,31,28,19,16},{14,13,2,1,30,29,18,17},{11,8,7,4,27,24,23,20},..., dimensions={0} | all-to-all | bytes 1048576 | tf_op jit(solution)/shard_map/all_to_all | solution.py:48
  155.1 0.0 copy-start.1
  155.1 2.8 gradient.3
  157.9 12.0 %all_to_all.80.in_ref = f32[8,64,256]{2,1,0:T(8,128)S(1)} all-to-all(f32[8,64,256]{2,1,0:T(8,128)S(1)} %gradient.3), channel_id=1, replica_groups={{15,14,11,10,63,62,59,58},{12,13,8,9,60,61,56,57},{3,2,7,6,51,50,55,54}..., dimensions={0} | all-to-all | bytes 1048576 | tf_op jit(solution)/shard_map/all_to_all | solution.py:48
  169.9 0.1 collective-permute-start
  170.0 1.2 collective-permute-done.other_ref
  171.2 0.0 copy-done.1
  171.2 0.1 first_step.1
  171.3 12.1 %all_to_all.81.in_ref = f32[8,136,128]{2,1,0:T(8,128)S(1)} all-to-all(f32[8,136,128]{2,1,0:T(8,128)S(1)} %get-tuple-element.42), channel_id=1, replica_groups={{15,14,11,10,63,62,59,58},{12,13,8,9,60,61,56,57},{3,2,7,6,51,50,55,54}..., dimensions={0} | all-to-all | bytes 1114112 | tf_op jit(solution)/shard_map/all_to_all | solution.py:48
  183.5 2.7 push.2
  186.2 13.3 %all_to_all.82.in_ref = f32[8,136,128]{2,1,0:T(8,128)S(1)} all-to-all(f32[8,136,128]{2,1,0:T(8,128)S(1)} %push.2), channel_id=1, replica_groups={{15,12,3,0,31,28,19,16},{14,13,2,1,30,29,18,17},{11,8,7,4,27,24,23,20},..., dimensions={0} | all-to-all | bytes 1114112 | tf_op jit(solution)/shard_map/all_to_all | solution.py:48
  199.5 0.2 next_residual.2
  199.7 13.2 %all_to_all.83.residual_ref = f32[8,128,128]{2,1,0:T(8,128)S(1)} all-to-all(f32[8,128,128]{2,1,0:T(8,128)S(1)} %get-tuple-element.46), channel_id=1, replica_groups={{15,12,3,0,31,28,19,16},{14,13,2,1,30,29,18,17},{11,8,7,4,27,24,23,20},..., dimensions={0} | all-to-all | bytes 1048576 | tf_op jit(solution)/shard_map/all_to_all | solution.py:48
  212.9 2.8 gradient.4
  215.7 12.0 %all_to_all.84.in_ref = f32[8,64,256]{2,1,0:T(8,128)S(1)} all-to-all(f32[8,64,256]{2,1,0:T(8,128)S(1)} %gradient.4), channel_id=1, replica_groups={{15,14,11,10,63,62,59,58},{12,13,8,9,60,61,56,57},{3,2,7,6,51,50,55,54}..., dimensions={0} | all-to-all | bytes 1048576 | tf_op jit(solution)/shard_map/all_to_all | solution.py:48
  227.7 0.1 collective-permute-start.1
  227.8 1.2 collective-permute-done.1.other_ref
  229.1 0.2 next_step.1
  229.3 12.1 %all_to_all.85.in_ref = f32[8,136,128]{2,1,0:T(8,128)S(1)} all-to-all(f32[8,136,128]{2,1,0:T(8,128)S(1)} %get-tuple-element.49), channel_id=1, replica_groups={{15,14,11,10,63,62,59,58},{12,13,8,9,60,61,56,57},{3,2,7,6,51,50,55,54}..., dimensions={0} | all-to-all | bytes 1114112 | tf_op jit(solution)/shard_map/all_to_all | solution.py:48
  241.4 2.7 push.3
  244.1 13.3 %all_to_all.86.in_ref = f32[8,136,128]{2,1,0:T(8,128)S(1)} all-to-all(f32[8,136,128]{2,1,0:T(8,128)S(1)} %push.3), channel_id=1, replica_groups={{15,12,3,0,31,28,19,16},{14,13,2,1,30,29,18,17},{11,8,7,4,27,24,23,20},..., dimensions={0} | all-to-all | bytes 1114112 | tf_op jit(solution)/shard_map/all_to_all | solution.py:48
  257.5 0.8 next_residual.3
  258.3 13.2 %all_to_all.87.residual_ref = f32[8,128,128]{2,1,0:T(8,128)S(1)} all-to-all(f32[8,128,128]{2,1,0:T(8,128)S(1)} %get-tuple-element.52), channel_id=1, replica_groups={{15,12,3,0,31,28,19,16},{14,13,2,1,30,29,18,17},{11,8,7,4,27,24,23,20},..., dimensions={0} | all-to-all | bytes 1048576 | tf_op jit(solution)/shard_map/all_to_all | solution.py:48
  271.5 2.8 gradient.5
  274.3 12.0 %all_to_all.88.in_ref = f32[8,64,256]{2,1,0:T(8,128)S(1)} all-to-all(f32[8,64,256]{2,1,0:T(8,128)S(1)} %gradient.5), channel_id=1, replica_groups={{15,14,11,10,63,62,59,58},{12,13,8,9,60,61,56,57},{3,2,7,6,51,50,55,54}..., dimensions={0} | all-to-all | bytes 1048576 | tf_op jit(solution)/shard_map/all_to_all | solution.py:48
  286.3 0.1 collective-permute-start.2
  286.4 1.2 collective-permute-done.2.other_ref
  287.6 0.2 last_gradient.1
  287.8 16.5 %all_to_all.89 = f32[64,1,128]{2,1,0:T(1,128)S(1)} all-to-all(f32[64,1,128]{2,1,0:T(1,128)S(1)} %bitcast.8), channel_id=1, replica_groups=mesh['rows'=2,'z'=4,'y'=4,'x'=4] {'z','y','x'}, dimensions={0} | all-to-all | bytes 65536 | tf_op jit(solution)/shard_map/all_to_all | solution.py:384
  304.3 0.8 close.1
  (6 shorter events, 0.1 us)
Async XLA Ops:
  0.0 105.4 %copy-start = (f32[64,256]{1,0:T(8,128)S(1)}, f32[64,256]{1,0:T(8,128)}, u32[]{:S(2)}) copy-start(f32[64,256]{1,0:T(8,128)} %anchor_ref.5) | copy-start | bytes 196612
  155.1 16.2 %copy-start.1 = (f32[256]{0:T(256)S(1)}, f32[256]{0:T(256)}, u32[]{:S(2)}) copy-start(f32[256]{0:T(256)} %param.7) | copy-start | bytes 3076
  169.9 1.3 collective-permute-start
  227.7 1.3 collective-permute-start.1
  286.3 1.3 collective-permute-start.2
where the time goes:
time: 306 us; the launch traced here: 305 us
  blocking collectives  273 us (89%)
  Pallas kernels  27.6 us (9%)
  waiting for transfers between devices  3.72 us (1%)
    all_to_all x13, blocking collectives, exchange(): lax.all_to_all(x, AXES, split_axis=0, concat_axis=0, axis_index_groups=gr...  257 us
    all_to_all x1, blocking collectives, body(): lax.all_to_all(squares, COLS, split_axis=0, concat_axis=0, tiled=True)  16.5 us
    pallas_call x1, Pallas kernels, opened(): pl.pallas_call(open_kernel, name='opened', out_shape=[array(CUBE, length...  11.5 us
    pallas_call x3, Pallas kernels, gradient_parts(): call(gradient_kernel, array(CUBE, samples, high.shape[1] // CUBE), 'gradi...  8.37 us
  transfers between devices with their start and end apart: 3, of which 3 were waited for; matrix products, arithmetic and copies ran while one was open for 0% of the time, Pallas kernels for 0%

commit v1 on v0

--- a/solution.py
+++ b/solution.py
@@ -11,7 +11,7 @@
 STEPS = 3
 SIDE = 4
 CUBE = 8
-SHIFT = (0, 1, 1)
+SHIFT = (1, 1, 0)
 AXES = ("rows", "z", "y", "x")
 COLS = ("z", "y", "x")
 LANES = 128
@@ -27,7 +27,12 @@
     turned = [(p + core + s) & (SIDE - 1) for p, s in zip(at, SHIFT)]
     half = [((t + 1) >> 1) & 1 for t in turned]
     pair = [t >> 1 for t in turned]
-    return half[0] * 4 + half[1] * 2 + half[2], pair[0] * 4 + pair[1] * 2 + pair[2]
+    return walk(half), walk(pair)
+
+
+def walk(bits):
+    a, b, c = bits
+    return a * 4 + (a ^ b) * 2 + (a ^ b ^ c)
 
 
 def cube_groups():
@@ -201,28 +206,30 @@
     )(parts, targets)
 
 
-def next_residual(parts, targets, logits, slope, samples, clip_level, params):
-    def kernel(in_ref, targets_ref, logits_ref, slope_ref, residual_ref, out_logits_ref, out_slope_ref, scale_ref):
+def next_residual(parts, targets, logits, slope, samples, clip_level, params, last):
+    def kernel(in_ref, targets_ref, logits_ref, slope_ref, residual_ref, scale_ref, *kept):
         length = targets_ref.shape[0]
         row = jnp.sum(in_ref[:, length:], axis=0)[:1]
         scale = scale_from(row, samples, clip_level, params)
         scale_ref[...] = jnp.broadcast_to(scale, scale_ref.shape)
         moved = jnp.sum(in_ref[:, :length], axis=0)
-        for t in range(length // samples):
-            at = slice(t * samples, (t + 1) * samples)
-            out_slope_ref[at] = 0.9 * slope_ref[at] + scale * moved[at]
-        logits = logits_ref[...] - 0.5 * out_slope_ref[...]
-        out_logits_ref[...] = logits
+        every = jnp.concatenate([scale] * (length // samples), 0)
+        slope = 0.9 * slope_ref[...] + every * moved
+        logits = logits_ref[...] - 0.5 * slope
+        if kept:
+            kept[0][...] = logits
+            kept[1][...] = slope
         residual_to(residual_ref, logits, targets_ref[...])
 
     shape = targets.shape
+    kept = 0 if last else 2
     return call(
         kernel,
-        [array(CUBE, *shape), array(*shape), array(*shape), array(samples, LANES)],
-        "next_residual",
+        [array(CUBE, *shape), array(samples, LANES)] + [array(*shape)] * kept,
+        "last_residual" if last else "next_residual",
         4,
         in_specs=[WHOLE] * 4,
-        out_specs=[WHOLE] * 4,
+        out_specs=[WHOLE] * (2 + kept),
     )(parts, targets, logits, slope)
 
 
@@ -378,7 +385,9 @@
         parts, gradient, *moved = stepped(gradient, other, prec, anchor, state)
         theta, velocity = moved if moved else (anchor, jnp.zeros_like(anchor))
         parts = exchange(push(exchange(parts, SECOND), *flips, samples), FIRST)
-        residual, logits, slope, scale = next_residual(parts, own, logits, slope, samples, clip_level, params)
+        last = step + 2 == STEPS
+        residual, scale, *kept = next_residual(parts, own, logits, slope, samples, clip_level, params, last)
+        logits, slope = kept or (None, None)
         state = (theta, velocity, gradient, scale)
     squares, gradient, theta, velocity = last_gradient(gradient, other, prec, anchor, state)
     squares = lax.all_to_all(squares, COLS, split_axis=0, concat_axis=0, tiled=True)

time: 306 us -> 302 us (0.987)
    all_to_all x13, blocking collectives: 257 us -> 253 us  [exchange(): lax.all_to_all(x, AXES, split_axis=0, concat_axis=0, axis_index_groups=gr...]
where the time goes in v1:
time: 302 us; the launch traced here: 301 us
  blocking collectives  270 us (89%)
  Pallas kernels  27.1 us (9%)
  waiting for transfers between devices  3.72 us (1%)
    all_to_all x13, blocking collectives, exchange(): lax.all_to_all(x, AXES, split_axis=0, concat_axis=0, axis_index_groups=gr...  253 us
    all_to_all x1, blocking collectives, body(): lax.all_to_all(squares, COLS, split_axis=0, concat_axis=0, tiled=True)  17.1 us
    pallas_call x1, Pallas kernels, opened(): pl.pallas_call(open_kernel, name='opened', out_shape=[array(CUBE, length...  11.5 us
    pallas_call x3, Pallas kernels, gradient_parts(): call(gradient_kernel, array(CUBE, samples, high.shape[1] // CUBE), 'gradi...  8.33 us
  transfers between devices with their start and end apart: 3, of which 3 were waited for; matrix products, arithmetic and copies ran while one was open for 0% of the time, Pallas kernels for 0%

profile of v1, /device:TPU:0, one launch (start us, length us, event | category | flops | bytes accessed | tf_op | source)
XLA Modules:
  0.0 301.1 jit_solution(7984296171496000348)
XLA Ops:
  0.0 0.0 copy-start
  0.0 103.8 %all_to_all.76.jac_ref = f32[8,2048,256]{2,1,0:T(8,128)} all-to-all(f32[8,2048,256]{2,1,0:T(8,128)} %bitcast.12), channel_id=1, replica_groups={{60,63,59,56,40,43,47,44},{61,62,58,57,41,42,46,45},{49,50,54,53,37,38,..., dimensions={0} | all-to-all | bytes 33554432 | tf_op jit(solution)/shard_map/all_to_all | solution.py:53
  103.8 0.0 copy-done
  103.9 11.3 %all_to_all.77.theta_ref = f32[8,64,256]{2,1,0:T(8,128)S(1)} all-to-all(f32[8,64,256]{2,1,0:T(8,128)S(1)} %broadcast_in_dim.15), channel_id=1, replica_groups={{60,63,59,56,40,43,47,44},{61,62,58,57,41,42,46,45},{49,50,54,53,37,38,..., dimensions={0} | all-to-all | bytes 1048576 | tf_op jit(solution)/shard_map/all_to_all | solution.py:53
  115.2 11.5 %opened.1 = (f32[8,136,128]{2,1,0:T(8,128)S(1)}, f32[128,128]{1,0:T(8,128)S(1)}, bf16[2048,2048]{1,0:T(8,128)(2,1)S(1)}, bf16[2048,2048]{1,0:T(8,128)(2,1)S(1)},...) custom-call(s32[1]{0:T(128)} %bitcast.at_ref, f32[64,16384]{1,0:T(8,128)} %targets_ref.1, ...), custom_call_target="tpu_custom_call" | custom-call | tf_op jit(solution)/shard_map/opened/pallas_call | solution.py:143
  126.7 15.0 %all_to_all.78.in_ref = f32[8,136,128]{2,1,0:T(8,128)S(1)} all-to-all(f32[8,136,128]{2,1,0:T(8,128)S(1)} %get-tuple-element.37), channel_id=1, replica_groups={{60,61,49,48,0,1,13,12},{63,62,50,51,3,2,14,15},{59,58,54,55,7,6,10,11}..., dimensions={0} | all-to-all | bytes 1114112 | tf_op jit(solution)/shard_map/all_to_all | solution.py:53
  141.7 0.1 first_residual.1
  141.8 12.8 %all_to_all.79.residual_ref = f32[8,128,128]{2,1,0:T(8,128)S(1)} all-to-all(f32[8,128,128]{2,1,0:T(8,128)S(1)} %get-tuple-element.39), channel_id=1, replica_groups={{60,61,49,48,0,1,13,12},{63,62,50,51,3,2,14,15},{59,58,54,55,7,6,10,11}..., dimensions={0} | all-to-all | bytes 1048576 | tf_op jit(solution)/shard_map/all_to_all | solution.py:53
  154.6 0.0 copy-start.1
  154.6 2.8 gradient.3
  157.4 11.3 %all_to_all.80.in_ref = f32[8,64,256]{2,1,0:T(8,128)S(1)} all-to-all(f32[8,64,256]{2,1,0:T(8,128)S(1)} %gradient.3), channel_id=1, replica_groups={{60,63,59,56,40,43,47,44},{61,62,58,57,41,42,46,45},{49,50,54,53,37,38,..., dimensions={0} | all-to-all | bytes 1048576 | tf_op jit(solution)/shard_map/all_to_all | solution.py:53
  168.7 0.1 collective-permute-start
  168.8 1.2 collective-permute-done.other_ref
  170.0 0.0 copy-done.1
  170.0 0.1 first_step.1
  170.1 12.2 %all_to_all.81.in_ref = f32[8,136,128]{2,1,0:T(8,128)S(1)} all-to-all(f32[8,136,128]{2,1,0:T(8,128)S(1)} %get-tuple-element.42), channel_id=1, replica_groups={{60,63,59,56,40,43,47,44},{61,62,58,57,41,42,46,45},{49,50,54,53,37,38,..., dimensions={0} | all-to-all | bytes 1114112 | tf_op jit(solution)/shard_map/all_to_all | solution.py:53
  182.3 2.7 push.2
  185.0 13.0 %all_to_all.82.in_ref = f32[8,136,128]{2,1,0:T(8,128)S(1)} all-to-all(f32[8,136,128]{2,1,0:T(8,128)S(1)} %push.2), channel_id=1, replica_groups={{60,61,49,48,0,1,13,12},{63,62,50,51,3,2,14,15},{59,58,54,55,7,6,10,11}..., dimensions={0} | all-to-all | bytes 1114112 | tf_op jit(solution)/shard_map/all_to_all | solution.py:53
  198.0 0.2 next_residual.1
  198.3 12.8 %all_to_all.83.residual_ref = f32[8,128,128]{2,1,0:T(8,128)S(1)} all-to-all(f32[8,128,128]{2,1,0:T(8,128)S(1)} %get-tuple-element.46), channel_id=1, replica_groups={{60,61,49,48,0,1,13,12},{63,62,50,51,3,2,14,15},{59,58,54,55,7,6,10,11}..., dimensions={0} | all-to-all | bytes 1048576 | tf_op jit(solution)/shard_map/all_to_all | solution.py:53
  211.1 2.8 gradient.4
  213.9 11.3 %all_to_all.84.in_ref = f32[8,64,256]{2,1,0:T(8,128)S(1)} all-to-all(f32[8,64,256]{2,1,0:T(8,128)S(1)} %gradient.4), channel_id=1, replica_groups={{60,63,59,56,40,43,47,44},{61,62,58,57,41,42,46,45},{49,50,54,53,37,38,..., dimensions={0} | all-to-all | bytes 1048576 | tf_op jit(solution)/shard_map/all_to_all | solution.py:53
  225.2 0.1 collective-permute-start.1
  225.3 1.2 collective-permute-done.1.other_ref
  226.6 0.2 next_step.1
  226.7 12.2 %all_to_all.85.in_ref = f32[8,136,128]{2,1,0:T(8,128)S(1)} all-to-all(f32[8,136,128]{2,1,0:T(8,128)S(1)} %get-tuple-element.49), channel_id=1, replica_groups={{60,63,59,56,40,43,47,44},{61,62,58,57,41,42,46,45},{49,50,54,53,37,38,..., dimensions={0} | all-to-all | bytes 1114112 | tf_op jit(solution)/shard_map/all_to_all | solution.py:53
  238.9 2.7 push.3
  241.6 12.9 %all_to_all.86.in_ref = f32[8,136,128]{2,1,0:T(8,128)S(1)} all-to-all(f32[8,136,128]{2,1,0:T(8,128)S(1)} %push.3), channel_id=1, replica_groups={{60,61,49,48,0,1,13,12},{63,62,50,51,3,2,14,15},{59,58,54,55,7,6,10,11}..., dimensions={0} | all-to-all | bytes 1114112 | tf_op jit(solution)/shard_map/all_to_all | solution.py:53
  254.6 0.2 last_residual.1
  254.8 12.8 %all_to_all.87.residual_ref = f32[8,128,128]{2,1,0:T(8,128)S(1)} all-to-all(f32[8,128,128]{2,1,0:T(8,128)S(1)} %get-tuple-element.52), channel_id=1, replica_groups={{60,61,49,48,0,1,13,12},{63,62,50,51,3,2,14,15},{59,58,54,55,7,6,10,11}..., dimensions={0} | all-to-all | bytes 1048576 | tf_op jit(solution)/shard_map/all_to_all | solution.py:53
  267.6 2.8 gradient.5
  270.4 11.3 %all_to_all.88.in_ref = f32[8,64,256]{2,1,0:T(8,128)S(1)} all-to-all(f32[8,64,256]{2,1,0:T(8,128)S(1)} %gradient.5), channel_id=1, replica_groups={{60,63,59,56,40,43,47,44},{61,62,58,57,41,42,46,45},{49,50,54,53,37,38,..., dimensions={0} | all-to-all | bytes 1048576 | tf_op jit(solution)/shard_map/all_to_all | solution.py:53
  281.8 0.1 collective-permute-start.2
  281.8 1.2 collective-permute-done.2.other_ref
  283.1 0.2 last_gradient.1
  283.3 17.1 %all_to_all.89 = f32[64,1,128]{2,1,0:T(1,128)S(1)} all-to-all(f32[64,1,128]{2,1,0:T(1,128)S(1)} %bitcast.8), channel_id=1, replica_groups=mesh['rows'=2,'z'=4,'y'=4,'x'=4] {'z','y','x'}, dimensions={0} | all-to-all | bytes 65536 | tf_op jit(solution)/shard_map/all_to_all | solution.py:393
  300.4 0.8 close.1
  (6 shorter events, 0.1 us)
Async XLA Ops:
  0.0 103.8 %copy-start = (f32[64,256]{1,0:T(8,128)S(1)}, f32[64,256]{1,0:T(8,128)}, u32[]{:S(2)}) copy-start(f32[64,256]{1,0:T(8,128)} %anchor_ref.5) | copy-start | bytes 196612
  154.6 15.4 %copy-start.1 = (f32[256]{0:T(256)S(1)}, f32[256]{0:T(256)}, u32[]{:S(2)}) copy-start(f32[256]{0:T(256)} %param.7) | copy-start | bytes 3076
  168.7 1.3 collective-permute-start
  225.2 1.3 collective-permute-start.1
  281.8 1.3 collective-permute-start.2

commit v2 on v1

--- a/solution.py
+++ b/solution.py
@@ -9,6 +9,7 @@
 from jax.sharding import PartitionSpec as P
 
 STEPS = 3
+SPLIT = (3, 3, 2)
 SIDE = 4
 CUBE = 8
 SHIFT = (1, 1, 0)
@@ -110,19 +111,9 @@
     out_ref[j, tiles * samples :] = tail
 
 
-def open_kernel(at_ref, targets_ref, theta_ref, jac_ref, out_ref, own_ref, *refs):
-    high_ref, low_ref, flip_high_ref, flip_low_ref, both_ref = refs
-    samples, cols = theta_ref.shape[1:]
+def split_kernel(jac_ref, high_ref, low_ref, flip_high_ref, flip_low_ref):
     j = pl.program_id(0)
-    part = jac_ref.shape[1]
-
-    @pl.when(j == 0)
-    def _():
-        for t in range(targets_ref.shape[1] // LANES):
-            own_ref[t * samples : (t + 1) * samples] = targets_ref[:, t * LANES : (t + 1) * LANES]
-        for c in range(CUBE):
-            both_ref[:, c * cols : (c + 1) * cols], _ = stacked(theta_ref[c])
-
+    _, part, cols = jac_ref.shape
     rows = pl.ds(pl.multiple_of(j * part, part), part)
     for c in range(CUBE):
         jac_high, jac_low = halves(jac_ref[c])
@@ -131,39 +122,80 @@
         low_ref[rows, at] = jac_low
         flip_high_ref[j, at] = jnp.transpose(jac_high)
         flip_low_ref[j, at] = jnp.transpose(jac_low)
+
+
+def split(jacobian, first, parts):
+    _, rows, cols = jacobian.shape
+    part = rows // CUBE
+    wide = CUBE * cols
+    return call(
+        split_kernel,
+        [array(parts * part, wide, dtype=BF16)] * 2 + [array(parts, wide, part, dtype=BF16)] * 2,
+        "split",
+        12,
+        grid=(parts,),
+        in_specs=[pl.BlockSpec((CUBE, part, cols), lambda j: (0, j + first, 0))],
+        out_specs=[WHOLE] * 4,
+    )(in_hbm(jacobian))
+
+
+def beside_kernel(own_ref, other_ref, out_ref):
+    members = own_ref.shape[0]
+    out_ref[:members] = own_ref[...]
+    out_ref[members:] = other_ref[...]
+
+
+def beside(own, other):
+    shape = (2 * own.shape[0], *own.shape[1:])
+    return call(beside_kernel, array(*shape), "beside", 4, in_specs=[WHOLE] * 2, out_specs=WHOLE)(own, other)
+
+
+def across(bit):
+    pairs = []
+    for group in SECOND:
+        for k in range(CUBE):
+            corner = (k ^ (k >> 1)) ^ (1 << bit)
+            pairs.append((group[k], group[walk((corner >> 2, corner >> 1 & 1, corner & 1))]))
+    return pairs
+
+
+def open_kernel(at_ref, targets_ref, theta_ref, *refs):
+    flips, (out_ref, own_ref, both_ref) = refs[:-3], refs[-3:]
+    samples, cols = theta_ref.shape[1:]
+    for t in range(targets_ref.shape[1] // LANES):
+        own_ref[t * samples : (t + 1) * samples] = targets_ref[:, t * LANES : (t + 1) * LANES]
+    for c in range(CUBE):
+        theta = theta_ref[(c ^ (c >> 1)) ^ at_ref[1]]
+        both_ref[:, c * cols : (c + 1) * cols], _ = stacked(theta)
     both = both_ref[...]
-    put_part(out_ref, 0, both, both[:samples], flip_high_ref[j], flip_low_ref[j], jnp.zeros((TAIL, LANES), F32))
-
-
-def opened(at, targets, theta, jacobian):
+    put_all(out_ref, both, both[:samples], flips, jnp.zeros((TAIL, LANES), F32))
+
+
+def put_all(out_ref, both, high, flips, tail):
+    j = 0
+    for high_ref, low_ref in zip(flips[::2], flips[1::2]):
+        for k in range(high_ref.shape[0]):
+            put_part(out_ref, j, both, high, high_ref[k], low_ref[k], tail)
+            j += 1
+
+
+def opened(at, targets, theta, flips):
     samples, cols = theta.shape[1:]
-    rows = jacobian.shape[1]
-    part = rows // CUBE
+    part = flips[0].shape[2]
     length = part // LANES * samples
     return pl.pallas_call(
         open_kernel,
         name="opened",
-        out_shape=[
-            array(CUBE, length + TAIL, LANES),
-            array(length, LANES),
-            array(rows, CUBE * cols, dtype=BF16),
-            array(rows, CUBE * cols, dtype=BF16),
-            array(CUBE, CUBE * cols, part, dtype=BF16),
-            array(CUBE, CUBE * cols, part, dtype=BF16),
-        ],
+        out_shape=[array(CUBE, length + TAIL, LANES), array(length, LANES)],
         grid_spec=pltpu.PrefetchScalarGridSpec(
             num_scalar_prefetch=1,
-            grid=(CUBE,),
-            in_specs=[
-                pl.BlockSpec((samples, part), lambda j, at: (0, at[0])),
-                WHOLE,
-                pl.BlockSpec((CUBE, part, cols), lambda j, at: (0, j, 0)),
-            ],
-            out_specs=[pl.BlockSpec((1, length + TAIL, LANES), lambda j, at: (j, 0, 0))] + [WHOLE] * 5,
+            grid=(1,),
+            in_specs=[pl.BlockSpec((samples, part), lambda j, at: (0, at[0]))] + [WHOLE] * (1 + len(flips)),
+            out_specs=[WHOLE] * 2,
             scratch_shapes=[pltpu.VMEM((2 * samples, CUBE * cols), BF16)],
         ),
-        compiler_params=pltpu.CompilerParams(vmem_limit_bytes=12 << 20),
-    )(at, in_hbm(targets), theta, in_hbm(jacobian))
+        compiler_params=pltpu.CompilerParams(vmem_limit_bytes=6 << 20),
+    )(at, in_hbm(targets), theta, *flips)
 
 
 def in_hbm(x):
@@ -238,24 +270,30 @@
     return jnp.concatenate([in_ref[b, t : t + samples] for b in range(blocks) for t in range(0, length, samples)], 1)
 
 
-def gradient_kernel(residual_ref, high_ref, low_ref, out_ref):
+def gradient_kernel(residual_ref, *refs):
+    jac, out_ref = refs[:-1], refs[-1]
     samples, cols = out_ref.shape[1:]
     both, high = stacked(joined(residual_ref, samples))
     for c in range(CUBE):
         at = slice(c * cols, (c + 1) * cols)
-        wide = dot(both, high_ref[:, at], DOWN)
-        out_ref[c] = wide[:samples] + wide[samples:] + dot(high, low_ref[:, at], DOWN)
-
-
-def gradient_parts(residual, high, low, samples):
+        total, row = 0.0, 0
+        for high_ref, low_ref in zip(jac[::2], jac[1::2]):
+            rows = slice(row, row + high_ref.shape[0])
+            wide = dot(both[:, rows], high_ref[:, at], DOWN)
+            total += wide[:samples] + wide[samples:] + dot(high[:, rows], low_ref[:, at], DOWN)
+            row = rows.stop
+        out_ref[c] = total
+
+
+def gradient_parts(residual, jac, samples):
     return call(
         gradient_kernel,
-        array(CUBE, samples, high.shape[1] // CUBE),
+        array(CUBE, samples, jac[0].shape[1] // CUBE),
         "gradient",
         6,
-        in_specs=[WHOLE] * 3,
+        in_specs=[WHOLE] * (1 + len(jac)),
         out_specs=WHOLE,
-    )(residual, high, low)
+    )(residual, *jac)
 
 
 def moved_on(state):
@@ -307,21 +345,19 @@
     )(own, other, prec, anchor, *state)
 
 
-def push(parts, flip_high, flip_low, samples):
-    def kernel(in_ref, high_ref, low_ref, out_ref):
+def push(parts, flips, samples):
+    def kernel(in_ref, *refs):
         both, first = stacked(joined(in_ref, samples))
-        tail = jnp.sum(in_ref[:, -TAIL:], axis=0)
-        for j in range(CUBE):
-            put_part(out_ref, j, both, first, high_ref[j], low_ref[j], tail)
+        put_all(refs[-1], both, first, refs[:-1], jnp.sum(in_ref[:, -TAIL:], axis=0))
 
     return call(
         kernel,
-        array(CUBE, flip_high.shape[2] // LANES * samples + TAIL, LANES),
+        array(CUBE, flips[0].shape[2] // LANES * samples + TAIL, LANES),
         "push",
         6,
-        in_specs=[WHOLE] * 3,
+        in_specs=[WHOLE] * (1 + len(flips)),
         out_specs=WHOLE,
-    )(parts, flip_high, flip_low)
+    )(parts, *flips)
 
 
 def last_kernel(own_ref, other_ref, prec_ref, anchor_ref, *refs):
@@ -366,25 +402,30 @@
     params = col_dev * SIDE**3
     clip_level = 0.2 * math.sqrt(row_dev * 2 / params)
     half, pair = own_block()
-    at = jnp.reshape(pair * CUBE + half, (1,)).astype(jnp.int32)
+    at = jnp.stack([pair * CUBE + half, pair ^ (pair >> 1)]).astype(jnp.int32)
     prec = precision[None, :]
     jacobian, at = lax.optimization_barrier((jacobian, at))
     square = exchange(jacobian.reshape(CUBE, row_dev // CUBE, col_dev), SECOND)
-    square, theta = lax.optimization_barrier((square, anchor))
-    theta = exchange(jnp.broadcast_to(theta[None], (CUBE, samples, col_dev)), SECOND)
-    parts, own, high, low, *flips = opened(at, targets, theta, square)
+    square, theta = lax.optimization_barrier((square, anchor[None]))
+    jac, flips, first = [], [], 0
+    for bit, parts in enumerate(SPLIT):
+        other = lax.ppermute(theta, AXES, across(bit))
+        other, square, high, low, *flip = lax.optimization_barrier((other, square, *split(square, first, parts)))
+        theta = beside(theta, other)
+        jac, flips, first = [*jac, high, low], [*flips, *flip], first + parts
+    parts, own = opened(at, targets, theta, flips)
     residual, logits = first_residual(exchange(parts, FIRST), own)
     slope = jnp.zeros_like(logits)
     state = ()
     for step in range(STEPS):
-        parts = gradient_parts(exchange(residual, FIRST), high, low, samples)
+        parts = gradient_parts(exchange(residual, FIRST), jac, samples)
         gradient = fold(exchange(parts, SECOND))
         other = lax.ppermute(gradient, "rows", [(0, 1), (1, 0)])
         if step + 1 == STEPS:
             break
         parts, gradient, *moved = stepped(gradient, other, prec, anchor, state)
         theta, velocity = moved if moved else (anchor, jnp.zeros_like(anchor))
-        parts = exchange(push(exchange(parts, SECOND), *flips, samples), FIRST)
+        parts = exchange(push(exchange(parts, SECOND), flips, samples), FIRST)
         last = step + 2 == STEPS
         residual, scale, *kept = next_residual(parts, own, logits, slope, samples, clip_level, params, last)
         logits, slope = kept or (None, None)

time: 302 us -> 303 us (level)
  blocking collectives: 270 us -> 260 us
  Pallas kernels: 27.1 us -> 32.6 us
    pallas_call x5 -> x11, Pallas kernels: 13.7 us -> 26.7 us  [the longest x3 12.4 us: split(): call(split_kernel, [array(parts * part, wide, dtype=BF16)] * 2 + [array(p...]
    all_to_all x13 -> x12, blocking collectives: 253 us -> 242 us  [exchange(): lax.all_to_all(x, AXES, split_axis=0, concat_axis=0, axis_index_groups=gr...]
    pallas_call x1, Pallas kernels: 11.5 us -> 4.11 us  [opened(): pl.pallas_call(open_kernel, name='opened', out_shape=[array(CUBE, length...]
  transfers between devices with their start and end apart: 3 -> 6, of which waited for: 3 -> 4; matrix products, arithmetic and copies ran while one was open for 0% -> 0% of each run, Pallas kernels for 0% -> 4%
where the time goes in v2:
time: 303 us; the launch traced here: 302 us
  blocking collectives  260 us (86%)
  Pallas kernels  32.6 us (11%)
  waiting for transfers between devices  6.63 us (2%)
    all_to_all x12, blocking collectives, exchange(): lax.all_to_all(x, AXES, split_axis=0, concat_axis=0, axis_index_groups=gr...  242 us
    all_to_all x1, blocking collectives, body(): lax.all_to_all(squares, COLS, split_axis=0, concat_axis=0, tiled=True)  17.1 us
    pallas_call x3, Pallas kernels, split(): call(split_kernel, [array(parts * part, wide, dtype=BF16)] * 2 + [array(p...  12.4 us
    pallas_call x3, Pallas kernels, gradient_parts(): call(gradient_kernel, array(CUBE, samples, jac[0].shape[1] // CUBE), 'gra...  8.8 us
  transfers between devices with their start and end apart: 6, of which 4 were waited for; matrix products, arithmetic and copies ran while one was open for 0% of the time, Pallas kernels for 4%

profile of v2, /device:TPU:0, one launch (start us, length us, event | category | flops | bytes accessed | tf_op | source)
XLA Modules:
  0.0 301.9 jit_solution(4936942625942400621)
XLA Ops:
  0.0 0.1 pad_add_fusion.at_ref
  0.1 0.0 copy-start
  0.1 103.8 %all_to_all.71.jac_ref = f32[8,2048,256]{2,1,0:T(8,128)} all-to-all(f32[8,2048,256]{2,1,0:T(8,128)} %bitcast.16), channel_id=1, replica_groups={{60,63,59,56,40,43,47,44},{61,62,58,57,41,42,46,45},{49,50,54,53,37,38,..., dimensions={0} | all-to-all | bytes 33554432 | tf_op jit(solution)/shard_map/all_to_all | solution.py:54
  103.9 0.0 copy-done
  103.9 1.3 collective-permute-start
  105.2 4.6 %split.3 = (bf16[768,2048]{1,0:T(8,128)(2,1)S(1)}, bf16[768,2048]{1,0:T(8,128)(2,1)S(1)}, bf16[3,2048,256]{2,1,0:T(8,128)(2,1)S(1)}, bf16[3,2048,256]{2,1,0:T(8,128)(2,1)S(1)}) custom-call(f32[8,2048,256]{2,1,0:T(8,128)} %all_to_all.71.jac_ref), custom_call_target="tpu_custom_call" | custom-call | tf_op jit(solution)/shard_map/split/pallas_call | solution.py:131
  109.9 0.0 collective-permute-done.other_ref
  109.9 0.7 collective-permute-start.1
  110.7 4.6 %split.4 = (bf16[768,2048]{1,0:T(8,128)(2,1)S(1)}, bf16[768,2048]{1,0:T(8,128)(2,1)S(1)}, bf16[3,2048,256]{2,1,0:T(8,128)(2,1)S(1)}, bf16[3,2048,256]{2,1,0:T(8,128)(2,1)S(1)}) custom-call(f32[8,2048,256]{2,1,0:T(8,128)} %all_to_all.71.jac_ref), custom_call_target="tpu_custom_call" | custom-call | tf_op jit(solution)/shard_map/split/pallas_call | solution.py:131
  115.3 0.0 collective-permute-done.1.other_ref
  115.3 0.5 collective-permute-start.2
  115.8 3.1 %split.5 = (bf16[512,2048]{1,0:T(8,128)(2,1)S(1)}, bf16[512,2048]{1,0:T(8,128)(2,1)S(1)}, bf16[2,2048,256]{2,1,0:T(8,128)(2,1)S(1)}, bf16[2,2048,256]{2,1,0:T(8,128)(2,1)S(1)}) custom-call(f32[8,2048,256]{2,1,0:T(8,128)} %all_to_all.71.jac_ref), custom_call_target="tpu_custom_call" | custom-call | tf_op jit(solution)/shard_map/split/pallas_call | solution.py:131
  118.9 2.9 collective-permute-done.2.other_ref
  121.8 4.1 %opened.1 = (f32[8,136,128]{2,1,0:T(8,128)S(1)}, f32[128,128]{1,0:T(8,128)S(1)}) custom-call(s32[2]{0:T(128)S(1)} %pad_add_fusion.at_ref, f32[64,16384]{1,0:T(8,128)} %targets_ref.1, f32[8,64,256]{2,1,0:T(8,128)S(1)} %beside.5.theta_ref, bf16[3,2048,256]{2,1,0:T(8,128)(2,1)S(1)} %get-tuple-element.79.refs_0_, ...), custom_call_target="tpu_custom_call" | custom-call | tf_op jit(solution)/shard_map/opened/pallas_call | solution.py:186
  126.0 15.0 %all_to_all.72.in_ref = f32[8,136,128]{2,1,0:T(8,128)S(1)} all-to-all(f32[8,136,128]{2,1,0:T(8,128)S(1)} %get-tuple-element.85), channel_id=1, replica_groups={{60,61,49,48,0,1,13,12},{63,62,50,51,3,2,14,15},{59,58,54,55,7,6,10,11}..., dimensions={0} | all-to-all | bytes 1114112 | tf_op jit(solution)/shard_map/all_to_all | solution.py:54
  140.9 0.1 first_residual.1
  141.0 12.8 %all_to_all.73.residual_ref = f32[8,128,128]{2,1,0:T(8,128)S(1)} all-to-all(f32[8,128,128]{2,1,0:T(8,128)S(1)} %get-tuple-element.87), channel_id=1, replica_groups={{60,61,49,48,0,1,13,12},{63,62,50,51,3,2,14,15},{59,58,54,55,7,6,10,11}..., dimensions={0} | all-to-all | bytes 1048576 | tf_op jit(solution)/shard_map/all_to_all | solution.py:54
  153.8 0.0 copy-start.1
  153.8 2.9 gradient.3
  156.8 12.4 %all_to_all.74.in_ref = f32[8,64,256]{2,1,0:T(8,128)S(1)} all-to-all(f32[8,64,256]{2,1,0:T(8,128)S(1)} %gradient.3), channel_id=1, replica_groups={{60,63,59,56,40,43,47,44},{61,62,58,57,41,42,46,45},{49,50,54,53,37,38,..., dimensions={0} | all-to-all | bytes 1048576 | tf_op jit(solution)/shard_map/all_to_all | solution.py:54
  169.2 0.1 collective-permute-start.3
  169.3 1.2 collective-permute-done.3.other_ref
  170.5 0.0 copy-done.1
  170.5 0.1 first_step.1
  170.6 12.2 %all_to_all.75.in_ref = f32[8,136,128]{2,1,0:T(8,128)S(1)} all-to-all(f32[8,136,128]{2,1,0:T(8,128)S(1)} %get-tuple-element.94), channel_id=1, replica_groups={{60,63,59,56,40,43,47,44},{61,62,58,57,41,42,46,45},{49,50,54,53,37,38,..., dimensions={0} | all-to-all | bytes 1114112 | tf_op jit(solution)/shard_map/all_to_all | solution.py:54
  182.8 2.7 push.2
  185.5 12.9 %all_to_all.76.in_ref = f32[8,136,128]{2,1,0:T(8,128)S(1)} all-to-all(f32[8,136,128]{2,1,0:T(8,128)S(1)} %push.2), channel_id=1, replica_groups={{60,61,49,48,0,1,13,12},{63,62,50,51,3,2,14,15},{59,58,54,55,7,6,10,11}..., dimensions={0} | all-to-all | bytes 1114112 | tf_op jit(solution)/shard_map/all_to_all | solution.py:54
  198.5 0.2 next_residual.1
  198.7 12.8 %all_to_all.77.residual_ref = f32[8,128,128]{2,1,0:T(8,128)S(1)} all-to-all(f32[8,128,128]{2,1,0:T(8,128)S(1)} %get-tuple-element.96), channel_id=1, replica_groups={{60,61,49,48,0,1,13,12},{63,62,50,51,3,2,14,15},{59,58,54,55,7,6,10,11}..., dimensions={0} | all-to-all | bytes 1048576 | tf_op jit(solution)/shard_map/all_to_all | solution.py:54
  211.5 2.9 gradient.4
  214.5 11.3 %all_to_all.78.in_ref = f32[8,64,256]{2,1,0:T(8,128)S(1)} all-to-all(f32[8,64,256]{2,1,0:T(8,128)S(1)} %gradient.4), channel_id=1, replica_groups={{60,63,59,56,40,43,47,44},{61,62,58,57,41,42,46,45},{49,50,54,53,37,38,..., dimensions={0} | all-to-all | bytes 1048576 | tf_op jit(solution)/shard_map/all_to_all | solution.py:54
  225.8 0.1 collective-permute-start.4
  225.9 1.2 collective-permute-done.4.other_ref
  227.1 0.2 next_step.1
  227.3 12.2 %all_to_all.79.in_ref = f32[8,136,128]{2,1,0:T(8,128)S(1)} all-to-all(f32[8,136,128]{2,1,0:T(8,128)S(1)} %get-tuple-element.99), channel_id=1, replica_groups={{60,63,59,56,40,43,47,44},{61,62,58,57,41,42,46,45},{49,50,54,53,37,38,..., dimensions={0} | all-to-all | bytes 1114112 | tf_op jit(solution)/shard_map/all_to_all | solution.py:54
  239.5 2.7 push.3
  242.2 13.0 %all_to_all.80.in_ref = f32[8,136,128]{2,1,0:T(8,128)S(1)} all-to-all(f32[8,136,128]{2,1,0:T(8,128)S(1)} %push.3), channel_id=1, replica_groups={{60,61,49,48,0,1,13,12},{63,62,50,51,3,2,14,15},{59,58,54,55,7,6,10,11}..., dimensions={0} | all-to-all | bytes 1114112 | tf_op jit(solution)/shard_map/all_to_all | solution.py:54
  255.2 0.2 last_residual.1
  255.4 12.8 %all_to_all.81.residual_ref = f32[8,128,128]{2,1,0:T(8,128)S(1)} all-to-all(f32[8,128,128]{2,1,0:T(8,128)S(1)} %get-tuple-element.102), channel_id=1, replica_groups={{60,61,49,48,0,1,13,12},{63,62,50,51,3,2,14,15},{59,58,54,55,7,6,10,11}..., dimensions={0} | all-to-all | bytes 1048576 | tf_op jit(solution)/shard_map/all_to_all | solution.py:54
  268.3 2.9 gradient.5
  271.2 11.3 %all_to_all.82.in_ref = f32[8,64,256]{2,1,0:T(8,128)S(1)} all-to-all(f32[8,64,256]{2,1,0:T(8,128)S(1)} %gradient.5), channel_id=1, replica_groups={{60,63,59,56,40,43,47,44},{61,62,58,57,41,42,46,45},{49,50,54,53,37,38,..., dimensions={0} | all-to-all | bytes 1048576 | tf_op jit(solution)/shard_map/all_to_all | solution.py:54
  282.5 0.1 collective-permute-start.5
  282.6 1.2 collective-permute-done.5.other_ref
  283.9 0.2 last_gradient.1
  284.0 17.1 %all_to_all.83 = f32[64,1,128]{2,1,0:T(1,128)S(1)} all-to-all(f32[64,1,128]{2,1,0:T(1,128)S(1)} %bitcast.12), channel_id=1, replica_groups=mesh['rows'=2,'z'=4,'y'=4,'x'=4] {'z','y','x'}, dimensions={0} | all-to-all | bytes 65536 | tf_op jit(solution)/shard_map/all_to_all | solution.py:434
  301.1 0.8 close.1
  (8 shorter events, 0.2 us)
Async XLA Ops:
  0.1 103.8 %copy-start = (f32[64,256]{1,0:T(8,128)S(1)}, f32[64,256]{1,0:T(8,128)}, u32[]{:S(2)}) copy-start(f32[64,256]{1,0:T(8,128)} %anchor_ref.5) | copy-start | bytes 196612
  103.9 6.0 %collective-permute-start = (f32[1,64,256]{2,1,0:T(8,128)S(1)}, f32[1,64,256]{2,1,0:T(8,128)S(1)}, u32[]{:S(2)}, u32[]{:S(2)}) collective-permute-start(f32[1,64,256]{2,1,0:T(8,128)S(1)} %bitcast.9), channel_id=1, source_target_pairs={{60,63},{63,60},{59,56},{56,59},{40,43},{43,40},{47,44},{44,47},{6... | collective-permute-start | bytes 196616 | tf_op jit(solution)/shard_map/ppermute | solution.py:412
  109.9 5.4 %collective-permute-start.1 = (f32[2,64,256]{2,1,0:T(8,128)S(1)}, f32[2,64,256]{2,1,0:T(8,128)S(1)}, u32[]{:S(2)}, u32[]{:S(2)}) collective-permute-start(f32[2,64,256]{2,1,0:T(8,128)S(1)} %beside.3.own_ref), channel_id=1, source_target_pairs={{60,56},{63,59},{59,63},{56,60},{40,44},{43,47},{47,43},{44,40},{6... | collective-permute-start | bytes 393224 | tf_op jit(solution)/shard_map/ppermute | solution.py:412
  115.3 6.5 %collective-permute-start.2 = (f32[4,64,256]{2,1,0:T(8,128)S(1)}, f32[4,64,256]{2,1,0:T(8,128)S(1)}, u32[]{:S(2)}, u32[]{:S(2)}) collective-permute-start(f32[4,64,256]{2,1,0:T(8,128)S(1)} %beside.4.own_ref), channel_id=1, source_target_pairs={{60,44},{63,47},{59,43},{56,40},{40,56},{43,59},{47,63},{44,60},{6... | collective-permute-start | bytes 786440 | tf_op jit(solution)/shard_map/ppermute | solution.py:412
  153.8 16.7 %copy-start.1 = (f32[256]{0:T(256)S(1)}, f32[256]{0:T(256)}, u32[]{:S(2)}) copy-start(f32[256]{0:T(256)} %param.7) | copy-start | bytes 3076
  169.2 1.3 collective-permute-start.3
  225.8 1.3 collective-permute-start.4
  282.5 1.3 collective-permute-start.5

commit v3 on v2

--- a/solution.py
+++ b/solution.py
@@ -9,7 +9,7 @@
 from jax.sharding import PartitionSpec as P
 
 STEPS = 3
-SPLIT = (3, 3, 2)
+SPLIT = (2, 3, 3)
 SIDE = 4
 CUBE = 8
 SHIFT = (1, 1, 0)
@@ -111,7 +111,13 @@
     out_ref[j, tiles * samples :] = tail
 
 
-def split_kernel(jac_ref, high_ref, low_ref, flip_high_ref, flip_low_ref):
+def split_kernel(at_ref, jac_ref, *refs):
+    if len(refs) > 4:
+        targets_ref, *refs, own_ref = refs
+        samples = targets_ref.shape[0]
+        for t in range(targets_ref.shape[1] // LANES):
+            own_ref[t * samples : (t + 1) * samples] = targets_ref[:, t * LANES : (t + 1) * LANES]
+    high_ref, low_ref, flip_high_ref, flip_low_ref = refs
     j = pl.program_id(0)
     _, part, cols = jac_ref.shape
     rows = pl.ds(pl.multiple_of(j * part, part), part)
@@ -124,19 +130,26 @@
         flip_low_ref[j, at] = jnp.transpose(jac_low)
 
 
-def split(jacobian, first, parts):
+def split(at, jacobian, first, parts, targets=()):
     _, rows, cols = jacobian.shape
     part = rows // CUBE
     wide = CUBE * cols
-    return call(
+    samples = [t.shape[0] for t in targets]
+    return pl.pallas_call(
         split_kernel,
-        [array(parts * part, wide, dtype=BF16)] * 2 + [array(parts, wide, part, dtype=BF16)] * 2,
-        "split",
-        12,
-        grid=(parts,),
-        in_specs=[pl.BlockSpec((CUBE, part, cols), lambda j: (0, j + first, 0))],
-        out_specs=[WHOLE] * 4,
-    )(in_hbm(jacobian))
+        name="split",
+        out_shape=[array(parts * part, wide, dtype=BF16)] * 2
+        + [array(parts, wide, part, dtype=BF16)] * 2
+        + [array(part // LANES * n, LANES) for n in samples],
+        grid_spec=pltpu.PrefetchScalarGridSpec(
+            num_scalar_prefetch=1,
+            grid=(parts,),
+            in_specs=[pl.BlockSpec((CUBE, part, cols), lambda j, at: (0, j + first, 0))]
+            + [pl.BlockSpec((n, part), lambda j, at: (0, at[0])) for n in samples],
+            out_specs=[WHOLE] * (4 + len(samples)),
+        ),
+        compiler_params=pltpu.CompilerParams(vmem_limit_bytes=12 << 20),
+    )(at, in_hbm(jacobian), *(in_hbm(t) for t in targets))
 
 
 def beside_kernel(own_ref, other_ref, out_ref):
@@ -159,11 +172,9 @@
     return pairs
 
 
-def open_kernel(at_ref, targets_ref, theta_ref, *refs):
-    flips, (out_ref, own_ref, both_ref) = refs[:-3], refs[-3:]
+def open_kernel(at_ref, theta_ref, *refs):
+    flips, (out_ref, both_ref) = refs[:-2], refs[-2:]
     samples, cols = theta_ref.shape[1:]
-    for t in range(targets_ref.shape[1] // LANES):
-        own_ref[t * samples : (t + 1) * samples] = targets_ref[:, t * LANES : (t + 1) * LANES]
     for c in range(CUBE):
         theta = theta_ref[(c ^ (c >> 1)) ^ at_ref[1]]
         both_ref[:, c * cols : (c + 1) * cols], _ = stacked(theta)
@@ -179,23 +190,18 @@
             j += 1
 
 
-def opened(at, targets, theta, flips):
+def opened(at, theta, flips):
     samples, cols = theta.shape[1:]
-    part = flips[0].shape[2]
-    length = part // LANES * samples
-    return pl.pallas_call(
+    length = flips[0].shape[2] // LANES * samples
+    return call(
         open_kernel,
-        name="opened",
-        out_shape=[array(CUBE, length + TAIL, LANES), array(length, LANES)],
-        grid_spec=pltpu.PrefetchScalarGridSpec(
-            num_scalar_prefetch=1,
-            grid=(1,),
-            in_specs=[pl.BlockSpec((samples, part), lambda j, at: (0, at[0]))] + [WHOLE] * (1 + len(flips)),
-            out_specs=[WHOLE] * 2,
-            scratch_shapes=[pltpu.VMEM((2 * samples, CUBE * cols), BF16)],
-        ),
-        compiler_params=pltpu.CompilerParams(vmem_limit_bytes=6 << 20),
-    )(at, in_hbm(targets), theta, *flips)
+        array(CUBE, length + TAIL, LANES),
+        "opened",
+        6,
+        in_specs=[pl.BlockSpec(memory_space=pltpu.SMEM)] + [WHOLE] * (1 + len(flips)),
+        out_specs=WHOLE,
+        scratch_shapes=[pltpu.VMEM((2 * samples, CUBE * cols), BF16)],
+    )(at, theta, *flips)
 
 
 def in_hbm(x):
@@ -410,10 +416,13 @@
     jac, flips, first = [], [], 0
     for bit, parts in enumerate(SPLIT):
         other = lax.ppermute(theta, AXES, across(bit))
-        other, square, high, low, *flip = lax.optimization_barrier((other, square, *split(square, first, parts)))
+        pieces = split(at, square, first, parts, () if bit else (targets,))
+        other, square, high, low, *flip = lax.optimization_barrier((other, square, *pieces))
+        if not bit:
+            *flip, own = flip
         theta = beside(theta, other)
         jac, flips, first = [*jac, high, low], [*flips, *flip], first + parts
-    parts, own = opened(at, targets, theta, flips)
+    parts = opened(at, theta, flips)
     residual, logits = first_residual(exchange(parts, FIRST), own)
     slope = jnp.zeros_like(logits)
     state = ()

time: 303 us -> 301 us (level)
  transfers between devices with their start and end apart: 6 -> 6, of which waited for: 4 -> 5; matrix products, arithmetic and copies ran while one was open for 0% -> 0% of each run, Pallas kernels for 4% -> 5%
where the time goes in v3:
time: 301 us
  blocking collectives  259 us (86%)
  Pallas kernels  33.6 us (11%)
  waiting for transfers between devices  5.21 us (2%)
  starting transfers between devices  3.03 us (1%)
    all_to_all x12, blocking collectives, exchange(): lax.all_to_all(x, AXES, split_axis=0, concat_axis=0, axis_index_groups=gr...  242 us
    all_to_all x1, blocking collectives, body(): lax.all_to_all(squares, COLS, split_axis=0, concat_axis=0, tiled=True)  17.1 us
    pallas_call x3, Pallas kernels, split(): pl.pallas_call(split_kernel, name='split', out_shape=[array(parts * part,...  14 us
    pallas_call x3, Pallas kernels, gradient_parts(): call(gradient_kernel, array(CUBE, samples, jac[0].shape[1] // CUBE), 'gra...  8.87 us
  transfers between devices with their start and end apart: 6, of which 5 were waited for; matrix products, arithmetic and copies ran while one was open for 0% of the time, Pallas kernels for 5%

profile of v3, /device:TPU:0, one launch (start us, length us, event | category | flops | bytes accessed | tf_op | source)
XLA Modules:
  0.0 300.7 jit_solution(3055745721009703552)
XLA Ops:
  0.0 0.1 pad_add_fusion.at_ref
  0.1 0.0 copy-start
  0.1 103.8 %all_to_all.71.jac_ref = f32[8,2048,256]{2,1,0:T(8,128)} all-to-all(f32[8,2048,256]{2,1,0:T(8,128)} %bitcast.16), channel_id=1, replica_groups={{60,63,59,56,40,43,47,44},{61,62,58,57,41,42,46,45},{49,50,54,53,37,38,..., dimensions={0} | all-to-all | bytes 33554432 | tf_op jit(solution)/shard_map/all_to_all | solution.py:54
  103.9 0.0 copy-done
  103.9 1.3 collective-permute-start
  105.3 3.6 %split.3 = (bf16[512,2048]{1,0:T(8,128)(2,1)S(1)}, bf16[512,2048]{1,0:T(8,128)(2,1)S(1)}, bf16[2,2048,256]{2,1,0:T(8,128)(2,1)S(1)}, bf16[2,2048,256]{2,1,0:T(8,128)(2,1)S(1)}, f32[128,128]{1,0:T(8,128)S(1)}) custom-call(s32[2]{0:T(128)S(1)} %pad_add_fusion.at_ref, f32[8,2048,256]{2,1,0:T(8,128)} %all_to_all.71.jac_ref, f32[64,16384]{1,0:T(8,128)} %refs_0_.2), custom_call_target="tpu_custom_call" | custom-call | tf_op jit(solution)/shard_map/split/pallas_call | solution.py:138
  108.9 0.5 collective-permute-done.other_ref
  109.4 1.2 collective-permute-start.1
  110.6 5.2 %split.4 = (bf16[768,2048]{1,0:T(8,128)(2,1)S(1)}, bf16[768,2048]{1,0:T(8,128)(2,1)S(1)}, bf16[3,2048,256]{2,1,0:T(8,128)(2,1)S(1)}, bf16[3,2048,256]{2,1,0:T(8,128)(2,1)S(1)}) custom-call(s32[2]{0:T(128)S(1)} %pad_add_fusion.at_ref, f32[8,2048,256]{2,1,0:T(8,128)} %all_to_all.71.jac_ref), custom_call_target="tpu_custom_call" | custom-call | tf_op jit(solution)/shard_map/split/pallas_call | solution.py:138
  115.8 0.0 collective-permute-done.1.other_ref
  115.8 0.3 collective-permute-start.2
  116.1 5.2 %split.5 = (bf16[768,2048]{1,0:T(8,128)(2,1)S(1)}, bf16[768,2048]{1,0:T(8,128)(2,1)S(1)}, bf16[3,2048,256]{2,1,0:T(8,128)(2,1)S(1)}, bf16[3,2048,256]{2,1,0:T(8,128)(2,1)S(1)}) custom-call(s32[2]{0:T(128)S(1)} %pad_add_fusion.at_ref, f32[8,2048,256]{2,1,0:T(8,128)} %all_to_all.71.jac_ref), custom_call_target="tpu_custom_call" | custom-call | tf_op jit(solution)/shard_map/split/pallas_call | solution.py:138
  121.3 1.0 collective-permute-done.2.other_ref
  122.3 3.3 %opened.1 = f32[8,136,128]{2,1,0:T(8,128)S(1)} custom-call(s32[2]{0:T(128)S(1)} %pad_add_fusion.at_ref, f32[8,64,256]{2,1,0:T(8,128)S(1)} %beside.5.theta_ref, bf16[2,2048,256]{2,1,0:T(8,128)(2,1)S(1)} %get-tuple-element.80.refs_0_, bf16[2,2048,256]{2,1,0:T(8,128)(2,1)S(1)} %get-tuple-element.81.refs_1_, ...), custom_call_target="tpu_custom_call" | custom-call | tf_op jit(solution)/shard_map/opened/pallas_call | solution.py:196
  125.6 15.0 %all_to_all.72.in_ref = f32[8,136,128]{2,1,0:T(8,128)S(1)} all-to-all(f32[8,136,128]{2,1,0:T(8,128)S(1)} %opened.1), channel_id=1, replica_groups={{60,61,49,48,0,1,13,12},{63,62,50,51,3,2,14,15},{59,58,54,55,7,6,10,11}..., dimensions={0} | all-to-all | bytes 1114112 | tf_op jit(solution)/shard_map/all_to_all | solution.py:54
  140.6 0.1 first_residual.1
  140.7 12.8 %all_to_all.73.residual_ref = f32[8,128,128]{2,1,0:T(8,128)S(1)} all-to-all(f32[8,128,128]{2,1,0:T(8,128)S(1)} %get-tuple-element.87), channel_id=1, replica_groups={{60,61,49,48,0,1,13,12},{63,62,50,51,3,2,14,15},{59,58,54,55,7,6,10,11}..., dimensions={0} | all-to-all | bytes 1048576 | tf_op jit(solution)/shard_map/all_to_all | solution.py:54
  153.5 0.0 copy-start.1
  153.5 3.0 gradient.3
  156.5 11.4 %all_to_all.74.in_ref = f32[8,64,256]{2,1,0:T(8,128)S(1)} all-to-all(f32[8,64,256]{2,1,0:T(8,128)S(1)} %gradient.3), channel_id=1, replica_groups={{60,63,59,56,40,43,47,44},{61,62,58,57,41,42,46,45},{49,50,54,53,37,38,..., dimensions={0} | all-to-all | bytes 1048576 | tf_op jit(solution)/shard_map/all_to_all | solution.py:54
  167.9 0.1 collective-permute-start.3
  168.0 1.2 collective-permute-done.3.other_ref
  169.2 0.0 copy-done.1
  169.2 0.1 first_step.1
  169.3 12.2 %all_to_all.75.in_ref = f32[8,136,128]{2,1,0:T(8,128)S(1)} all-to-all(f32[8,136,128]{2,1,0:T(8,128)S(1)} %get-tuple-element.94), channel_id=1, replica_groups={{60,63,59,56,40,43,47,44},{61,62,58,57,41,42,46,45},{49,50,54,53,37,38,..., dimensions={0} | all-to-all | bytes 1114112 | tf_op jit(solution)/shard_map/all_to_all | solution.py:54
  181.5 2.8 push.2
  184.3 13.0 %all_to_all.76.in_ref = f32[8,136,128]{2,1,0:T(8,128)S(1)} all-to-all(f32[8,136,128]{2,1,0:T(8,128)S(1)} %push.2), channel_id=1, replica_groups={{60,61,49,48,0,1,13,12},{63,62,50,51,3,2,14,15},{59,58,54,55,7,6,10,11}..., dimensions={0} | all-to-all | bytes 1114112 | tf_op jit(solution)/shard_map/all_to_all | solution.py:54
  197.2 0.2 next_residual.1
  197.5 12.8 %all_to_all.77.residual_ref = f32[8,128,128]{2,1,0:T(8,128)S(1)} all-to-all(f32[8,128,128]{2,1,0:T(8,128)S(1)} %get-tuple-element.96), channel_id=1, replica_groups={{60,61,49,48,0,1,13,12},{63,62,50,51,3,2,14,15},{59,58,54,55,7,6,10,11}..., dimensions={0} | all-to-all | bytes 1048576 | tf_op jit(solution)/shard_map/all_to_all | solution.py:54
  210.3 3.0 gradient.4
  213.2 11.3 %all_to_all.78.in_ref = f32[8,64,256]{2,1,0:T(8,128)S(1)} all-to-all(f32[8,64,256]{2,1,0:T(8,128)S(1)} %gradient.4), channel_id=1, replica_groups={{60,63,59,56,40,43,47,44},{61,62,58,57,41,42,46,45},{49,50,54,53,37,38,..., dimensions={0} | all-to-all | bytes 1048576 | tf_op jit(solution)/shard_map/all_to_all | solution.py:54
  224.6 0.1 collective-permute-start.4
  224.7 1.2 collective-permute-done.4.other_ref
  225.9 0.2 next_step.1
  226.1 12.2 %all_to_all.79.in_ref = f32[8,136,128]{2,1,0:T(8,128)S(1)} all-to-all(f32[8,136,128]{2,1,0:T(8,128)S(1)} %get-tuple-element.99), channel_id=1, replica_groups={{60,63,59,56,40,43,47,44},{61,62,58,57,41,42,46,45},{49,50,54,53,37,38,..., dimensions={0} | all-to-all | bytes 1114112 | tf_op jit(solution)/shard_map/all_to_all | solution.py:54
  238.3 2.7 push.3
  241.0 13.0 %all_to_all.80.in_ref = f32[8,136,128]{2,1,0:T(8,128)S(1)} all-to-all(f32[8,136,128]{2,1,0:T(8,128)S(1)} %push.3), channel_id=1, replica_groups={{60,61,49,48,0,1,13,12},{63,62,50,51,3,2,14,15},{59,58,54,55,7,6,10,11}..., dimensions={0} | all-to-all | bytes 1114112 | tf_op jit(solution)/shard_map/all_to_all | solution.py:54
  254.0 0.2 last_residual.1
  254.2 12.8 %all_to_all.81.residual_ref = f32[8,128,128]{2,1,0:T(8,128)S(1)} all-to-all(f32[8,128,128]{2,1,0:T(8,128)S(1)} %get-tuple-element.102), channel_id=1, replica_groups={{60,61,49,48,0,1,13,12},{63,62,50,51,3,2,14,15},{59,58,54,55,7,6,10,11}..., dimensions={0} | all-to-all | bytes 1048576 | tf_op jit(solution)/shard_map/all_to_all | solution.py:54
  267.0 3.0 gradient.5
  270.0 11.3 %all_to_all.82.in_ref = f32[8,64,256]{2,1,0:T(8,128)S(1)} all-to-all(f32[8,64,256]{2,1,0:T(8,128)S(1)} %gradient.5), channel_id=1, replica_groups={{60,63,59,56,40,43,47,44},{61,62,58,57,41,42,46,45},{49,50,54,53,37,38,..., dimensions={0} | all-to-all | bytes 1048576 | tf_op jit(solution)/shard_map/all_to_all | solution.py:54
  281.3 0.1 collective-permute-start.5
  281.4 1.2 collective-permute-done.5.other_ref
  282.7 0.2 last_gradient.1
  282.8 17.1 %all_to_all.83 = f32[64,1,128]{2,1,0:T(1,128)S(1)} all-to-all(f32[64,1,128]{2,1,0:T(1,128)S(1)} %bitcast.12), channel_id=1, replica_groups=mesh['rows'=2,'z'=4,'y'=4,'x'=4] {'z','y','x'}, dimensions={0} | all-to-all | bytes 65536 | tf_op jit(solution)/shard_map/all_to_all | solution.py:443
  299.9 0.8 close.1
  (8 shorter events, 0.2 us)
Async XLA Ops:
  0.1 103.8 %copy-start = (f32[64,256]{1,0:T(8,128)S(1)}, f32[64,256]{1,0:T(8,128)}, u32[]{:S(2)}) copy-start(f32[64,256]{1,0:T(8,128)} %anchor_ref.5) | copy-start | bytes 196612
  103.9 5.5 %collective-permute-start = (f32[1,64,256]{2,1,0:T(8,128)S(1)}, f32[1,64,256]{2,1,0:T(8,128)S(1)}, u32[]{:S(2)}, u32[]{:S(2)}) collective-permute-start(f32[1,64,256]{2,1,0:T(8,128)S(1)} %bitcast.9), channel_id=1, source_target_pairs={{60,63},{63,60},{59,56},{56,59},{40,43},{43,40},{47,44},{44,47},{6... | collective-permute-start | bytes 196616 | tf_op jit(solution)/shard_map/ppermute | solution.py:418
  109.4 6.4 %collective-permute-start.1 = (f32[2,64,256]{2,1,0:T(8,128)S(1)}, f32[2,64,256]{2,1,0:T(8,128)S(1)}, u32[]{:S(2)}, u32[]{:S(2)}) collective-permute-start(f32[2,64,256]{2,1,0:T(8,128)S(1)} %beside.3.own_ref), channel_id=1, source_target_pairs={{60,56},{63,59},{59,63},{56,60},{40,44},{43,47},{47,43},{44,40},{6... | collective-permute-start | bytes 393224 | tf_op jit(solution)/shard_map/ppermute | solution.py:418
  115.8 6.5 %collective-permute-start.2 = (f32[4,64,256]{2,1,0:T(8,128)S(1)}, f32[4,64,256]{2,1,0:T(8,128)S(1)}, u32[]{:S(2)}, u32[]{:S(2)}) collective-permute-start(f32[4,64,256]{2,1,0:T(8,128)S(1)} %beside.4.own_ref), channel_id=1, source_target_pairs={{60,44},{63,47},{59,43},{56,40},{40,56},{43,59},{47,63},{44,60},{6... | collective-permute-start | bytes 786440 | tf_op jit(solution)/shard_map/ppermute | solution.py:418
  153.5 15.7 %copy-start.1 = (f32[256]{0:T(256)S(1)}, f32[256]{0:T(256)}, u32[]{:S(2)}) copy-start(f32[256]{0:T(256)} %param.7) | copy-start | bytes 3076
  167.9 1.3 collective-permute-start.3
  224.6 1.3 collective-permute-start.4
  281.3 1.3 collective-permute-start.5

commit v4 on v3

--- a/solution.py
+++ b/solution.py
@@ -28,12 +28,16 @@
     turned = [(p + core + s) & (SIDE - 1) for p, s in zip(at, SHIFT)]
     half = [((t + 1) >> 1) & 1 for t in turned]
     pair = [t >> 1 for t in turned]
-    return walk(half), walk(pair)
-
-
-def walk(bits):
+    return number(half), number(pair)
+
+
+def number(bits):
     a, b, c = bits
-    return a * 4 + (a ^ b) * 2 + (a ^ b ^ c)
+    return (a ^ b) * 4 + (a ^ c) * 2 + a
+
+
+def corner_of(k):
+    return (k & 1) * 4 + ((k >> 1) ^ (3 * (k & 1)))
 
 
 def cube_groups():
@@ -167,8 +171,8 @@
     pairs = []
     for group in SECOND:
         for k in range(CUBE):
-            corner = (k ^ (k >> 1)) ^ (1 << bit)
-            pairs.append((group[k], group[walk((corner >> 2, corner >> 1 & 1, corner & 1))]))
+            corner = corner_of(k) ^ (1 << bit)
+            pairs.append((group[k], group[number((corner >> 2, corner >> 1 & 1, corner & 1))]))
     return pairs
 
 
@@ -176,7 +180,7 @@
     flips, (out_ref, both_ref) = refs[:-2], refs[-2:]
     samples, cols = theta_ref.shape[1:]
     for c in range(CUBE):
-        theta = theta_ref[(c ^ (c >> 1)) ^ at_ref[1]]
+        theta = theta_ref[corner_of(c) ^ at_ref[1]]
         both_ref[:, c * cols : (c + 1) * cols], _ = stacked(theta)
     both = both_ref[...]
     put_all(out_ref, both, both[:samples], flips, jnp.zeros((TAIL, LANES), F32))
@@ -408,7 +412,7 @@
     params = col_dev * SIDE**3
     clip_level = 0.2 * math.sqrt(row_dev * 2 / params)
     half, pair = own_block()
-    at = jnp.stack([pair * CUBE + half, pair ^ (pair >> 1)]).astype(jnp.int32)
+    at = jnp.stack([pair * CUBE + half, corner_of(pair)]).astype(jnp.int32)
     prec = precision[None, :]
     jacobian, at = lax.optimization_barrier((jacobian, at))
     square = exchange(jacobian.reshape(CUBE, row_dev // CUBE, col_dev), SECOND)

time: 301 us -> 300 us (level)
  transfers between devices with their start and end apart: 6 -> 6, of which waited for: 5 -> 4; matrix products, arithmetic and copies ran while one was open for 0% -> 0% of each run, Pallas kernels for 5% -> 5%
where the time goes in v4:
time: 300 us; the launch traced here: 299 us
  blocking collectives  257 us (86%)
  Pallas kernels  33.6 us (11%)
  waiting for transfers between devices  4.77 us (2%)
  starting transfers between devices  3.39 us (1%)
    all_to_all x12, blocking collectives, exchange(): lax.all_to_all(x, AXES, split_axis=0, concat_axis=0, axis_index_groups=gr...  240 us
    all_to_all x1, blocking collectives, body(): lax.all_to_all(squares, COLS, split_axis=0, concat_axis=0, tiled=True)  16.5 us
    pallas_call x3, Pallas kernels, split(): pl.pallas_call(split_kernel, name='split', out_shape=[array(parts * part,...  14 us
    pallas_call x3, Pallas kernels, gradient_parts(): call(gradient_kernel, array(CUBE, samples, jac[0].shape[1] // CUBE), 'gra...  8.87 us
  transfers between devices with their start and end apart: 6, of which 4 were waited for; matrix products, arithmetic and copies ran while one was open for 0% of the time, Pallas kernels for 5%

profile of v4, /device:TPU:0, one launch (start us, length us, event | category | flops | bytes accessed | tf_op | source)
XLA Modules:
  0.0 298.9 jit_solution(9610373111825455066)
XLA Ops:
  0.0 0.1 pad_add_fusion.at_ref
  0.1 0.0 copy-start
  0.1 103.5 %all_to_all.71.jac_ref = f32[8,2048,256]{2,1,0:T(8,128)} all-to-all(f32[8,2048,256]{2,1,0:T(8,128)} %bitcast.16), channel_id=1, replica_groups={{60,43,63,40,56,47,59,44},{1,22,2,21,5,18,6,17},{61,42,62,41,57,46,58,4..., dimensions={0} | all-to-all | bytes 33554432 | tf_op jit(solution)/shard_map/all_to_all | solution.py:58
  103.6 0.0 copy-done
  103.6 0.8 collective-permute-start
  104.4 3.6 %split.3 = (bf16[512,2048]{1,0:T(8,128)(2,1)S(1)}, bf16[512,2048]{1,0:T(8,128)(2,1)S(1)}, bf16[2,2048,256]{2,1,0:T(8,128)(2,1)S(1)}, bf16[2,2048,256]{2,1,0:T(8,128)(2,1)S(1)}, f32[128,128]{1,0:T(8,128)S(1)}) custom-call(s32[2]{0:T(128)S(1)} %pad_add_fusion.at_ref, f32[8,2048,256]{2,1,0:T(8,128)} %all_to_all.71.jac_ref, f32[64,16384]{1,0:T(8,128)} %refs_0_.2), custom_call_target="tpu_custom_call" | custom-call | tf_op jit(solution)/shard_map/split/pallas_call | solution.py:142
  108.0 1.0 collective-permute-done.other_ref
  109.0 1.0 collective-permute-start.1
  110.0 5.2 %split.4 = (bf16[768,2048]{1,0:T(8,128)(2,1)S(1)}, bf16[768,2048]{1,0:T(8,128)(2,1)S(1)}, bf16[3,2048,256]{2,1,0:T(8,128)(2,1)S(1)}, bf16[3,2048,256]{2,1,0:T(8,128)(2,1)S(1)}) custom-call(s32[2]{0:T(128)S(1)} %pad_add_fusion.at_ref, f32[8,2048,256]{2,1,0:T(8,128)} %all_to_all.71.jac_ref), custom_call_target="tpu_custom_call" | custom-call | tf_op jit(solution)/shard_map/split/pallas_call | solution.py:142
  115.2 0.0 collective-permute-done.1.other_ref
  115.3 1.3 collective-permute-start.2
  116.6 5.2 %split.5 = (bf16[768,2048]{1,0:T(8,128)(2,1)S(1)}, bf16[768,2048]{1,0:T(8,128)(2,1)S(1)}, bf16[3,2048,256]{2,1,0:T(8,128)(2,1)S(1)}, bf16[3,2048,256]{2,1,0:T(8,128)(2,1)S(1)}) custom-call(s32[2]{0:T(128)S(1)} %pad_add_fusion.at_ref, f32[8,2048,256]{2,1,0:T(8,128)} %all_to_all.71.jac_ref), custom_call_target="tpu_custom_call" | custom-call | tf_op jit(solution)/shard_map/split/pallas_call | solution.py:142
  121.8 0.0 collective-permute-done.2.other_ref
  121.9 3.3 %opened.1 = f32[8,136,128]{2,1,0:T(8,128)S(1)} custom-call(s32[2]{0:T(128)S(1)} %pad_add_fusion.at_ref, f32[8,64,256]{2,1,0:T(8,128)S(1)} %beside.5.theta_ref, bf16[2,2048,256]{2,1,0:T(8,128)(2,1)S(1)} %get-tuple-element.80.refs_0_, bf16[2,2048,256]{2,1,0:T(8,128)(2,1)S(1)} %get-tuple-element.81.refs_1_, ...), custom_call_target="tpu_custom_call" | custom-call | tf_op jit(solution)/shard_map/opened/pallas_call | solution.py:200
  125.2 14.9 %all_to_all.72.in_ref = f32[8,136,128]{2,1,0:T(8,128)S(1)} all-to-all(f32[8,136,128]{2,1,0:T(8,128)S(1)} %opened.1), channel_id=1, replica_groups={{60,1,61,0,48,13,49,12},{43,22,42,23,39,26,38,27},{63,2,62,3,51,14,50,1..., dimensions={0} | all-to-all | bytes 1114112 | tf_op jit(solution)/shard_map/all_to_all | solution.py:58
  140.1 0.1 first_residual.1
  140.2 13.1 %all_to_all.73.residual_ref = f32[8,128,128]{2,1,0:T(8,128)S(1)} all-to-all(f32[8,128,128]{2,1,0:T(8,128)S(1)} %get-tuple-element.87), channel_id=1, replica_groups={{60,1,61,0,48,13,49,12},{43,22,42,23,39,26,38,27},{63,2,62,3,51,14,50,1..., dimensions={0} | all-to-all | bytes 1048576 | tf_op jit(solution)/shard_map/all_to_all | solution.py:58
  153.3 0.0 copy-start.1
  153.3 3.0 gradient.3
  156.2 11.0 %all_to_all.74.in_ref = f32[8,64,256]{2,1,0:T(8,128)S(1)} all-to-all(f32[8,64,256]{2,1,0:T(8,128)S(1)} %gradient.3), channel_id=1, replica_groups={{60,43,63,40,56,47,59,44},{1,22,2,21,5,18,6,17},{61,42,62,41,57,46,58,4..., dimensions={0} | all-to-all | bytes 1048576 | tf_op jit(solution)/shard_map/all_to_all | solution.py:58
  167.3 0.1 collective-permute-start.3
  167.4 1.2 collective-permute-done.3.other_ref
  168.6 0.0 copy-done.1
  168.6 0.1 first_step.1
  168.7 12.3 %all_to_all.75.in_ref = f32[8,136,128]{2,1,0:T(8,128)S(1)} all-to-all(f32[8,136,128]{2,1,0:T(8,128)S(1)} %get-tuple-element.94), channel_id=1, replica_groups={{60,43,63,40,56,47,59,44},{1,22,2,21,5,18,6,17},{61,42,62,41,57,46,58,4..., dimensions={0} | all-to-all | bytes 1114112 | tf_op jit(solution)/shard_map/all_to_all | solution.py:58
  181.0 2.7 push.2
  183.8 12.6 %all_to_all.76.in_ref = f32[8,136,128]{2,1,0:T(8,128)S(1)} all-to-all(f32[8,136,128]{2,1,0:T(8,128)S(1)} %push.2), channel_id=1, replica_groups={{60,1,61,0,48,13,49,12},{43,22,42,23,39,26,38,27},{63,2,62,3,51,14,50,1..., dimensions={0} | all-to-all | bytes 1114112 | tf_op jit(solution)/shard_map/all_to_all | solution.py:58
  196.4 0.2 next_residual.1
  196.6 13.1 %all_to_all.77.residual_ref = f32[8,128,128]{2,1,0:T(8,128)S(1)} all-to-all(f32[8,128,128]{2,1,0:T(8,128)S(1)} %get-tuple-element.96), channel_id=1, replica_groups={{60,1,61,0,48,13,49,12},{43,22,42,23,39,26,38,27},{63,2,62,3,51,14,50,1..., dimensions={0} | all-to-all | bytes 1048576 | tf_op jit(solution)/shard_map/all_to_all | solution.py:58
  209.7 3.0 gradient.4
  212.7 10.9 %all_to_all.78.in_ref = f32[8,64,256]{2,1,0:T(8,128)S(1)} all-to-all(f32[8,64,256]{2,1,0:T(8,128)S(1)} %gradient.4), channel_id=1, replica_groups={{60,43,63,40,56,47,59,44},{1,22,2,21,5,18,6,17},{61,42,62,41,57,46,58,4..., dimensions={0} | all-to-all | bytes 1048576 | tf_op jit(solution)/shard_map/all_to_all | solution.py:58
  223.6 0.1 collective-permute-start.4
  223.7 1.2 collective-permute-done.4.other_ref
  225.0 0.2 next_step.1
  225.2 12.3 %all_to_all.79.in_ref = f32[8,136,128]{2,1,0:T(8,128)S(1)} all-to-all(f32[8,136,128]{2,1,0:T(8,128)S(1)} %get-tuple-element.99), channel_id=1, replica_groups={{60,43,63,40,56,47,59,44},{1,22,2,21,5,18,6,17},{61,42,62,41,57,46,58,4..., dimensions={0} | all-to-all | bytes 1114112 | tf_op jit(solution)/shard_map/all_to_all | solution.py:58
  237.5 2.8 push.3
  240.3 12.6 %all_to_all.80.in_ref = f32[8,136,128]{2,1,0:T(8,128)S(1)} all-to-all(f32[8,136,128]{2,1,0:T(8,128)S(1)} %push.3), channel_id=1, replica_groups={{60,1,61,0,48,13,49,12},{43,22,42,23,39,26,38,27},{63,2,62,3,51,14,50,1..., dimensions={0} | all-to-all | bytes 1114112 | tf_op jit(solution)/shard_map/all_to_all | solution.py:58
  252.9 0.2 last_residual.1
  253.1 13.1 %all_to_all.81.residual_ref = f32[8,128,128]{2,1,0:T(8,128)S(1)} all-to-all(f32[8,128,128]{2,1,0:T(8,128)S(1)} %get-tuple-element.102), channel_id=1, replica_groups={{60,1,61,0,48,13,49,12},{43,22,42,23,39,26,38,27},{63,2,62,3,51,14,50,1..., dimensions={0} | all-to-all | bytes 1048576 | tf_op jit(solution)/shard_map/all_to_all | solution.py:58
  266.2 3.0 gradient.5
  269.2 10.9 %all_to_all.82.in_ref = f32[8,64,256]{2,1,0:T(8,128)S(1)} all-to-all(f32[8,64,256]{2,1,0:T(8,128)S(1)} %gradient.5), channel_id=1, replica_groups={{60,43,63,40,56,47,59,44},{1,22,2,21,5,18,6,17},{61,42,62,41,57,46,58,4..., dimensions={0} | all-to-all | bytes 1048576 | tf_op jit(solution)/shard_map/all_to_all | solution.py:58
  280.1 0.1 collective-permute-start.5
  280.2 1.2 collective-permute-done.5.other_ref
  281.5 0.2 last_gradient.1
  281.6 16.5 %all_to_all.83 = f32[64,1,128]{2,1,0:T(1,128)S(1)} all-to-all(f32[64,1,128]{2,1,0:T(1,128)S(1)} %bitcast.12), channel_id=1, replica_groups=mesh['rows'=2,'z'=4,'y'=4,'x'=4] {'z','y','x'}, dimensions={0} | all-to-all | bytes 65536 | tf_op jit(solution)/shard_map/all_to_all | solution.py:447
  298.1 0.8 close.1
  (8 shorter events, 0.2 us)
Async XLA Ops:
  0.1 103.5 %copy-start = (f32[64,256]{1,0:T(8,128)S(1)}, f32[64,256]{1,0:T(8,128)}, u32[]{:S(2)}) copy-start(f32[64,256]{1,0:T(8,128)} %anchor_ref.5) | copy-start | bytes 196612
  103.6 5.5 %collective-permute-start = (f32[1,64,256]{2,1,0:T(8,128)S(1)}, f32[1,64,256]{2,1,0:T(8,128)S(1)}, u32[]{:S(2)}, u32[]{:S(2)}) collective-permute-start(f32[1,64,256]{2,1,0:T(8,128)S(1)} %bitcast.9), channel_id=1, source_target_pairs={{60,63},{43,40},{63,60},{40,43},{56,59},{47,44},{59,56},{44,47},{1... | collective-permute-start | bytes 196616 | tf_op jit(solution)/shard_map/ppermute | solution.py:422
  109.0 6.2 %collective-permute-start.1 = (f32[2,64,256]{2,1,0:T(8,128)S(1)}, f32[2,64,256]{2,1,0:T(8,128)S(1)}, u32[]{:S(2)}, u32[]{:S(2)}) collective-permute-start(f32[2,64,256]{2,1,0:T(8,128)S(1)} %beside.3.own_ref), channel_id=1, source_target_pairs={{60,56},{43,47},{63,59},{40,44},{56,60},{47,43},{59,63},{44,40},{1... | collective-permute-start | bytes 393224 | tf_op jit(solution)/shard_map/ppermute | solution.py:422
  115.3 6.6 %collective-permute-start.2 = (f32[4,64,256]{2,1,0:T(8,128)S(1)}, f32[4,64,256]{2,1,0:T(8,128)S(1)}, u32[]{:S(2)}, u32[]{:S(2)}) collective-permute-start(f32[4,64,256]{2,1,0:T(8,128)S(1)} %beside.4.own_ref), channel_id=1, source_target_pairs={{60,44},{43,59},{63,47},{40,56},{56,40},{47,63},{59,43},{44,60},{1... | collective-permute-start | bytes 786440 | tf_op jit(solution)/shard_map/ppermute | solution.py:422
  153.3 15.4 %copy-start.1 = (f32[256]{0:T(256)S(1)}, f32[256]{0:T(256)}, u32[]{:S(2)}) copy-start(f32[256]{0:T(256)} %param.7) | copy-start | bytes 3076
  167.3 1.3 collective-permute-start.3
  223.6 1.3 collective-permute-start.4
  280.1 1.3 collective-permute-start.5

commit v5 on v4

--- a/solution.py
+++ b/solution.py
@@ -51,7 +51,16 @@
     return in_order(first), in_order(second)
 
 
+def everyone():
+    pairs = []
+    for chip in range(SIDE**3 // 2):
+        z, y, x = chip // 16, chip // 4 % 4, chip % 4
+        pairs += [chip, (z ^ 2) * 16 + (y ^ 2) * 4 + (x ^ 2)]
+    return [[core * SIDE**3 + chip for chip in pairs] for core in range(2)]
+
+
 FIRST, SECOND = cube_groups()
+ALL = everyone()
 
 
 def exchange(x, groups):
@@ -444,7 +453,7 @@
         logits, slope = kept or (None, None)
         state = (theta, velocity, gradient, scale)
     squares, gradient, theta, velocity = last_gradient(gradient, other, prec, anchor, state)
-    squares = lax.all_to_all(squares, COLS, split_axis=0, concat_axis=0, tiled=True)
+    squares = exchange(squares, ALL)
     return close(squares, theta, velocity, gradient, clip_level, params)
 
 

time: 300 us -> 299 us (level)
    all_to_all x1 -> x0, blocking collectives: 16.5 us -> none  [body(): lax.all_to_all(squares, COLS, split_axis=0, concat_axis=0, tiled=True)]
    all_to_all x12 -> x13, blocking collectives: 240 us -> 257 us  [exchange(): lax.all_to_all(x, AXES, split_axis=0, concat_axis=0, axis_index_groups=gr...]
where the time goes in v5:
time: 299 us
  blocking collectives  257 us (86%)
  Pallas kernels  33.6 us (11%)
  waiting for transfers between devices  4.77 us (2%)
  starting transfers between devices  3.39 us (1%)
    all_to_all x13, blocking collectives, exchange(): lax.all_to_all(x, AXES, split_axis=0, concat_axis=0, axis_index_groups=gr...  257 us
    pallas_call x3, Pallas kernels, split(): pl.pallas_call(split_kernel, name='split', out_shape=[array(parts * part,...  14 us
    pallas_call x3, Pallas kernels, gradient_parts(): call(gradient_kernel, array(CUBE, samples, jac[0].shape[1] // CUBE), 'gra...  8.87 us
  transfers between devices with their start and end apart: 6, of which 4 were waited for; matrix products, arithmetic and copies ran while one was open for 0% of the time, Pallas kernels for 5%

profile of v5, /device:TPU:0, one launch (start us, length us, event | category | flops | bytes accessed | tf_op | source)
XLA Modules:
  0.0 298.7 jit_solution(17477811690416553393)
XLA Ops:
  0.0 0.1 pad_add_fusion.at_ref
  0.1 0.0 copy-start
  0.1 103.5 %all_to_all.71.jac_ref = f32[8,2048,256]{2,1,0:T(8,128)} all-to-all(f32[8,2048,256]{2,1,0:T(8,128)} %bitcast.16), channel_id=1, replica_groups={{60,43,63,40,56,47,59,44},{1,22,2,21,5,18,6,17},{61,42,62,41,57,46,58,4..., dimensions={0} | all-to-all | bytes 33554432 | tf_op jit(solution)/shard_map/all_to_all | solution.py:67
  103.6 0.0 copy-done
  103.6 0.8 collective-permute-start
  104.4 3.6 %split.3 = (bf16[512,2048]{1,0:T(8,128)(2,1)S(1)}, bf16[512,2048]{1,0:T(8,128)(2,1)S(1)}, bf16[2,2048,256]{2,1,0:T(8,128)(2,1)S(1)}, bf16[2,2048,256]{2,1,0:T(8,128)(2,1)S(1)}, f32[128,128]{1,0:T(8,128)S(1)}) custom-call(s32[2]{0:T(128)S(1)} %pad_add_fusion.at_ref, f32[8,2048,256]{2,1,0:T(8,128)} %all_to_all.71.jac_ref, f32[64,16384]{1,0:T(8,128)} %refs_0_.2), custom_call_target="tpu_custom_call" | custom-call | tf_op jit(solution)/shard_map/split/pallas_call | solution.py:151
  108.0 1.0 collective-permute-done.other_ref
  109.0 1.0 collective-permute-start.1
  110.0 5.2 %split.4 = (bf16[768,2048]{1,0:T(8,128)(2,1)S(1)}, bf16[768,2048]{1,0:T(8,128)(2,1)S(1)}, bf16[3,2048,256]{2,1,0:T(8,128)(2,1)S(1)}, bf16[3,2048,256]{2,1,0:T(8,128)(2,1)S(1)}) custom-call(s32[2]{0:T(128)S(1)} %pad_add_fusion.at_ref, f32[8,2048,256]{2,1,0:T(8,128)} %all_to_all.71.jac_ref), custom_call_target="tpu_custom_call" | custom-call | tf_op jit(solution)/shard_map/split/pallas_call | solution.py:151
  115.2 0.0 collective-permute-done.1.other_ref
  115.3 1.3 collective-permute-start.2
  116.6 5.2 %split.5 = (bf16[768,2048]{1,0:T(8,128)(2,1)S(1)}, bf16[768,2048]{1,0:T(8,128)(2,1)S(1)}, bf16[3,2048,256]{2,1,0:T(8,128)(2,1)S(1)}, bf16[3,2048,256]{2,1,0:T(8,128)(2,1)S(1)}) custom-call(s32[2]{0:T(128)S(1)} %pad_add_fusion.at_ref, f32[8,2048,256]{2,1,0:T(8,128)} %all_to_all.71.jac_ref), custom_call_target="tpu_custom_call" | custom-call | tf_op jit(solution)/shard_map/split/pallas_call | solution.py:151
  121.8 0.0 collective-permute-done.2.other_ref
  121.9 3.3 %opened.1 = f32[8,136,128]{2,1,0:T(8,128)S(1)} custom-call(s32[2]{0:T(128)S(1)} %pad_add_fusion.at_ref, f32[8,64,256]{2,1,0:T(8,128)S(1)} %beside.5.theta_ref, bf16[2,2048,256]{2,1,0:T(8,128)(2,1)S(1)} %get-tuple-element.80.refs_0_, bf16[2,2048,256]{2,1,0:T(8,128)(2,1)S(1)} %get-tuple-element.81.refs_1_, ...), custom_call_target="tpu_custom_call" | custom-call | tf_op jit(solution)/shard_map/opened/pallas_call | solution.py:209
  125.2 14.9 %all_to_all.72.in_ref = f32[8,136,128]{2,1,0:T(8,128)S(1)} all-to-all(f32[8,136,128]{2,1,0:T(8,128)S(1)} %opened.1), channel_id=1, replica_groups={{60,1,61,0,48,13,49,12},{43,22,42,23,39,26,38,27},{63,2,62,3,51,14,50,1..., dimensions={0} | all-to-all | bytes 1114112 | tf_op jit(solution)/shard_map/all_to_all | solution.py:67
  140.1 0.1 first_residual.1
  140.2 13.1 %all_to_all.73.residual_ref = f32[8,128,128]{2,1,0:T(8,128)S(1)} all-to-all(f32[8,128,128]{2,1,0:T(8,128)S(1)} %get-tuple-element.87), channel_id=1, replica_groups={{60,1,61,0,48,13,49,12},{43,22,42,23,39,26,38,27},{63,2,62,3,51,14,50,1..., dimensions={0} | all-to-all | bytes 1048576 | tf_op jit(solution)/shard_map/all_to_all | solution.py:67
  153.3 0.0 copy-start.1
  153.3 3.0 gradient.3
  156.2 11.0 %all_to_all.74.in_ref = f32[8,64,256]{2,1,0:T(8,128)S(1)} all-to-all(f32[8,64,256]{2,1,0:T(8,128)S(1)} %gradient.3), channel_id=1, replica_groups={{60,43,63,40,56,47,59,44},{1,22,2,21,5,18,6,17},{61,42,62,41,57,46,58,4..., dimensions={0} | all-to-all | bytes 1048576 | tf_op jit(solution)/shard_map/all_to_all | solution.py:67
  167.3 0.1 collective-permute-start.3
  167.4 1.2 collective-permute-done.3.other_ref
  168.6 0.0 copy-done.1
  168.6 0.1 first_step.1
  168.7 12.3 %all_to_all.75.in_ref = f32[8,136,128]{2,1,0:T(8,128)S(1)} all-to-all(f32[8,136,128]{2,1,0:T(8,128)S(1)} %get-tuple-element.94), channel_id=1, replica_groups={{60,43,63,40,56,47,59,44},{1,22,2,21,5,18,6,17},{61,42,62,41,57,46,58,4..., dimensions={0} | all-to-all | bytes 1114112 | tf_op jit(solution)/shard_map/all_to_all | solution.py:67
  181.0 2.7 push.2
  183.8 12.6 %all_to_all.76.in_ref = f32[8,136,128]{2,1,0:T(8,128)S(1)} all-to-all(f32[8,136,128]{2,1,0:T(8,128)S(1)} %push.2), channel_id=1, replica_groups={{60,1,61,0,48,13,49,12},{43,22,42,23,39,26,38,27},{63,2,62,3,51,14,50,1..., dimensions={0} | all-to-all | bytes 1114112 | tf_op jit(solution)/shard_map/all_to_all | solution.py:67
  196.4 0.2 next_residual.1
  196.6 13.1 %all_to_all.77.residual_ref = f32[8,128,128]{2,1,0:T(8,128)S(1)} all-to-all(f32[8,128,128]{2,1,0:T(8,128)S(1)} %get-tuple-element.96), channel_id=1, replica_groups={{60,1,61,0,48,13,49,12},{43,22,42,23,39,26,38,27},{63,2,62,3,51,14,50,1..., dimensions={0} | all-to-all | bytes 1048576 | tf_op jit(solution)/shard_map/all_to_all | solution.py:67
  209.7 3.0 gradient.4
  212.7 10.9 %all_to_all.78.in_ref = f32[8,64,256]{2,1,0:T(8,128)S(1)} all-to-all(f32[8,64,256]{2,1,0:T(8,128)S(1)} %gradient.4), channel_id=1, replica_groups={{60,43,63,40,56,47,59,44},{1,22,2,21,5,18,6,17},{61,42,62,41,57,46,58,4..., dimensions={0} | all-to-all | bytes 1048576 | tf_op jit(solution)/shard_map/all_to_all | solution.py:67
  223.6 0.1 collective-permute-start.4
  223.7 1.2 collective-permute-done.4.other_ref
  225.0 0.2 next_step.1
  225.2 12.3 %all_to_all.79.in_ref = f32[8,136,128]{2,1,0:T(8,128)S(1)} all-to-all(f32[8,136,128]{2,1,0:T(8,128)S(1)} %get-tuple-element.99), channel_id=1, replica_groups={{60,43,63,40,56,47,59,44},{1,22,2,21,5,18,6,17},{61,42,62,41,57,46,58,4..., dimensions={0} | all-to-all | bytes 1114112 | tf_op jit(solution)/shard_map/all_to_all | solution.py:67
  237.5 2.8 push.3
  240.3 12.6 %all_to_all.80.in_ref = f32[8,136,128]{2,1,0:T(8,128)S(1)} all-to-all(f32[8,136,128]{2,1,0:T(8,128)S(1)} %push.3), channel_id=1, replica_groups={{60,1,61,0,48,13,49,12},{43,22,42,23,39,26,38,27},{63,2,62,3,51,14,50,1..., dimensions={0} | all-to-all | bytes 1114112 | tf_op jit(solution)/shard_map/all_to_all | solution.py:67
  252.9 0.2 last_residual.1
  253.1 13.1 %all_to_all.81.residual_ref = f32[8,128,128]{2,1,0:T(8,128)S(1)} all-to-all(f32[8,128,128]{2,1,0:T(8,128)S(1)} %get-tuple-element.102), channel_id=1, replica_groups={{60,1,61,0,48,13,49,12},{43,22,42,23,39,26,38,27},{63,2,62,3,51,14,50,1..., dimensions={0} | all-to-all | bytes 1048576 | tf_op jit(solution)/shard_map/all_to_all | solution.py:67
  266.2 3.0 gradient.5
  269.2 10.9 %all_to_all.82.in_ref = f32[8,64,256]{2,1,0:T(8,128)S(1)} all-to-all(f32[8,64,256]{2,1,0:T(8,128)S(1)} %gradient.5), channel_id=1, replica_groups={{60,43,63,40,56,47,59,44},{1,22,2,21,5,18,6,17},{61,42,62,41,57,46,58,4..., dimensions={0} | all-to-all | bytes 1048576 | tf_op jit(solution)/shard_map/all_to_all | solution.py:67
  280.1 0.1 collective-permute-start.5
  280.2 1.2 collective-permute-done.5.other_ref
  281.5 0.2 last_gradient.1
  281.6 16.3 %all_to_all.83 = f32[64,1,128]{2,1,0:T(1,128)S(1)} all-to-all(f32[64,1,128]{2,1,0:T(1,128)S(1)} %bitcast.12), channel_id=1, replica_groups={{0,42,1,43,2,40,3,41,4,46,5,47,6,44,7,45,8,34,9,35,10,32,11,33,12,38,13..., dimensions={0} | all-to-all | bytes 65536 | tf_op jit(solution)/shard_map/all_to_all | solution.py:67
  297.9 0.8 close.1
  (8 shorter events, 0.2 us)
Async XLA Ops:
  0.1 103.5 %copy-start = (f32[64,256]{1,0:T(8,128)S(1)}, f32[64,256]{1,0:T(8,128)}, u32[]{:S(2)}) copy-start(f32[64,256]{1,0:T(8,128)} %anchor_ref.5) | copy-start | bytes 196612
  103.6 5.5 %collective-permute-start = (f32[1,64,256]{2,1,0:T(8,128)S(1)}, f32[1,64,256]{2,1,0:T(8,128)S(1)}, u32[]{:S(2)}, u32[]{:S(2)}) collective-permute-start(f32[1,64,256]{2,1,0:T(8,128)S(1)} %bitcast.9), channel_id=1, source_target_pairs={{60,63},{43,40},{63,60},{40,43},{56,59},{47,44},{59,56},{44,47},{1... | collective-permute-start | bytes 196616 | tf_op jit(solution)/shard_map/ppermute | solution.py:431
  109.0 6.2 %collective-permute-start.1 = (f32[2,64,256]{2,1,0:T(8,128)S(1)}, f32[2,64,256]{2,1,0:T(8,128)S(1)}, u32[]{:S(2)}, u32[]{:S(2)}) collective-permute-start(f32[2,64,256]{2,1,0:T(8,128)S(1)} %beside.3.own_ref), channel_id=1, source_target_pairs={{60,56},{43,47},{63,59},{40,44},{56,60},{47,43},{59,63},{44,40},{1... | collective-permute-start | bytes 393224 | tf_op jit(solution)/shard_map/ppermute | solution.py:431
  115.3 6.6 %collective-permute-start.2 = (f32[4,64,256]{2,1,0:T(8,128)S(1)}, f32[4,64,256]{2,1,0:T(8,128)S(1)}, u32[]{:S(2)}, u32[]{:S(2)}) collective-permute-start(f32[4,64,256]{2,1,0:T(8,128)S(1)} %beside.4.own_ref), channel_id=1, source_target_pairs={{60,44},{43,59},{63,47},{40,56},{56,40},{47,63},{59,43},{44,60},{1... | collective-permute-start | bytes 786440 | tf_op jit(solution)/shard_map/ppermute | solution.py:431
  153.3 15.4 %copy-start.1 = (f32[256]{0:T(256)S(1)}, f32[256]{0:T(256)}, u32[]{:S(2)}) copy-start(f32[256]{0:T(256)} %param.7) | copy-start | bytes 3076
  167.3 1.3 collective-permute-start.3
  223.6 1.3 collective-permute-start.4
  280.1 1.3 collective-permute-start.5

commit v6 on v5

--- a/solution.py
+++ b/solution.py
@@ -9,7 +9,7 @@
 from jax.sharding import PartitionSpec as P
 
 STEPS = 3
-SPLIT = (2, 3, 3)
+SPLIT = (2, 2, 4)
 SIDE = 4
 CUBE = 8
 SHIFT = (1, 1, 0)

time: 299 us -> 299 us (level)
  transfers between devices with their start and end apart: 6 -> 6, of which waited for: 4 -> 5; matrix products, arithmetic and copies ran while one was open for 0% -> 0% of each run, Pallas kernels for 5% -> 4%
where the time goes in v6:
time: 299 us
  blocking collectives  257 us (86%)
  Pallas kernels  32.8 us (11%)
  waiting for transfers between devices  5.2 us (2%)
  starting transfers between devices  3.52 us (1%)
    all_to_all x13, blocking collectives, exchange(): lax.all_to_all(x, AXES, split_axis=0, concat_axis=0, axis_index_groups=gr...  257 us
    pallas_call x3, Pallas kernels, split(): pl.pallas_call(split_kernel, name='split', out_shape=[array(parts * part,...  13.3 us
    pallas_call x3, Pallas kernels, gradient_parts(): call(gradient_kernel, array(CUBE, samples, jac[0].shape[1] // CUBE), 'gra...  8.79 us
  transfers between devices with their start and end apart: 6, of which 5 were waited for; matrix products, arithmetic and copies ran while one was open for 0% of the time, Pallas kernels for 4%

profile of v6, /device:TPU:0, one launch (start us, length us, event | category | flops | bytes accessed | tf_op | source)
XLA Modules:
  0.0 298.6 jit_solution(4219966202058859028)
XLA Ops:
  0.0 0.1 pad_add_fusion.at_ref
  0.1 0.0 copy-start
  0.1 103.5 %all_to_all.71.jac_ref = f32[8,2048,256]{2,1,0:T(8,128)} all-to-all(f32[8,2048,256]{2,1,0:T(8,128)} %bitcast.16), channel_id=1, replica_groups={{60,43,63,40,56,47,59,44},{1,22,2,21,5,18,6,17},{61,42,62,41,57,46,58,4..., dimensions={0} | all-to-all | bytes 33554432 | tf_op jit(solution)/shard_map/all_to_all | solution.py:67
  103.6 0.0 copy-done
  103.6 0.8 collective-permute-start
  104.4 3.6 %split.3 = (bf16[512,2048]{1,0:T(8,128)(2,1)S(1)}, bf16[512,2048]{1,0:T(8,128)(2,1)S(1)}, bf16[2,2048,256]{2,1,0:T(8,128)(2,1)S(1)}, bf16[2,2048,256]{2,1,0:T(8,128)(2,1)S(1)}, f32[128,128]{1,0:T(8,128)S(1)}) custom-call(s32[2]{0:T(128)S(1)} %pad_add_fusion.at_ref, f32[8,2048,256]{2,1,0:T(8,128)} %all_to_all.71.jac_ref, f32[64,16384]{1,0:T(8,128)} %refs_0_.2), custom_call_target="tpu_custom_call" | custom-call | tf_op jit(solution)/shard_map/split/pallas_call | solution.py:151
  108.0 1.0 collective-permute-done.other_ref
  109.0 1.0 collective-permute-start.1
  110.0 3.6 %split.4 = (bf16[512,2048]{1,0:T(8,128)(2,1)S(1)}, bf16[512,2048]{1,0:T(8,128)(2,1)S(1)}, bf16[2,2048,256]{2,1,0:T(8,128)(2,1)S(1)}, bf16[2,2048,256]{2,1,0:T(8,128)(2,1)S(1)}) custom-call(s32[2]{0:T(128)S(1)} %pad_add_fusion.at_ref, f32[8,2048,256]{2,1,0:T(8,128)} %all_to_all.71.jac_ref), custom_call_target="tpu_custom_call" | custom-call | tf_op jit(solution)/shard_map/split/pallas_call | solution.py:151
  113.7 0.4 collective-permute-done.1.other_ref
  114.1 1.5 collective-permute-start.2
  115.6 6.1 %split.5 = (bf16[1024,2048]{1,0:T(8,128)(2,1)S(1)}, bf16[1024,2048]{1,0:T(8,128)(2,1)S(1)}, bf16[4,2048,256]{2,1,0:T(8,128)(2,1)S(1)}, bf16[4,2048,256]{2,1,0:T(8,128)(2,1)S(1)}) custom-call(s32[2]{0:T(128)S(1)} %pad_add_fusion.at_ref, f32[8,2048,256]{2,1,0:T(8,128)} %all_to_all.71.jac_ref), custom_call_target="tpu_custom_call" | custom-call | tf_op jit(solution)/shard_map/split/pallas_call | solution.py:151
  121.7 0.0 collective-permute-done.2.other_ref
  121.7 3.3 %opened.1 = f32[8,136,128]{2,1,0:T(8,128)S(1)} custom-call(s32[2]{0:T(128)S(1)} %pad_add_fusion.at_ref, f32[8,64,256]{2,1,0:T(8,128)S(1)} %beside.5.theta_ref, bf16[2,2048,256]{2,1,0:T(8,128)(2,1)S(1)} %get-tuple-element.80.refs_0_, bf16[2,2048,256]{2,1,0:T(8,128)(2,1)S(1)} %get-tuple-element.81.refs_1_, ...), custom_call_target="tpu_custom_call" | custom-call | tf_op jit(solution)/shard_map/opened/pallas_call | solution.py:209
  125.0 15.2 %all_to_all.72.in_ref = f32[8,136,128]{2,1,0:T(8,128)S(1)} all-to-all(f32[8,136,128]{2,1,0:T(8,128)S(1)} %opened.1), channel_id=1, replica_groups={{60,1,61,0,48,13,49,12},{43,22,42,23,39,26,38,27},{63,2,62,3,51,14,50,1..., dimensions={0} | all-to-all | bytes 1114112 | tf_op jit(solution)/shard_map/all_to_all | solution.py:67
  140.2 0.1 first_residual.1
  140.2 13.1 %all_to_all.73.residual_ref = f32[8,128,128]{2,1,0:T(8,128)S(1)} all-to-all(f32[8,128,128]{2,1,0:T(8,128)S(1)} %get-tuple-element.87), channel_id=1, replica_groups={{60,1,61,0,48,13,49,12},{43,22,42,23,39,26,38,27},{63,2,62,3,51,14,50,1..., dimensions={0} | all-to-all | bytes 1048576 | tf_op jit(solution)/shard_map/all_to_all | solution.py:67
  153.3 0.0 copy-start.1
  153.3 2.9 gradient.3
  156.2 11.0 %all_to_all.74.in_ref = f32[8,64,256]{2,1,0:T(8,128)S(1)} all-to-all(f32[8,64,256]{2,1,0:T(8,128)S(1)} %gradient.3), channel_id=1, replica_groups={{60,43,63,40,56,47,59,44},{1,22,2,21,5,18,6,17},{61,42,62,41,57,46,58,4..., dimensions={0} | all-to-all | bytes 1048576 | tf_op jit(solution)/shard_map/all_to_all | solution.py:67
  167.3 0.1 collective-permute-start.3
  167.4 1.2 collective-permute-done.3.other_ref
  168.6 0.0 copy-done.1
  168.6 0.1 first_step.1
  168.8 12.3 %all_to_all.75.in_ref = f32[8,136,128]{2,1,0:T(8,128)S(1)} all-to-all(f32[8,136,128]{2,1,0:T(8,128)S(1)} %get-tuple-element.94), channel_id=1, replica_groups={{60,43,63,40,56,47,59,44},{1,22,2,21,5,18,6,17},{61,42,62,41,57,46,58,4..., dimensions={0} | all-to-all | bytes 1114112 | tf_op jit(solution)/shard_map/all_to_all | solution.py:67
  181.1 2.7 push.2
  183.8 12.6 %all_to_all.76.in_ref = f32[8,136,128]{2,1,0:T(8,128)S(1)} all-to-all(f32[8,136,128]{2,1,0:T(8,128)S(1)} %push.2), channel_id=1, replica_groups={{60,1,61,0,48,13,49,12},{43,22,42,23,39,26,38,27},{63,2,62,3,51,14,50,1..., dimensions={0} | all-to-all | bytes 1114112 | tf_op jit(solution)/shard_map/all_to_all | solution.py:67
  196.4 0.2 next_residual.1
  196.7 13.1 %all_to_all.77.residual_ref = f32[8,128,128]{2,1,0:T(8,128)S(1)} all-to-all(f32[8,128,128]{2,1,0:T(8,128)S(1)} %get-tuple-element.96), channel_id=1, replica_groups={{60,1,61,0,48,13,49,12},{43,22,42,23,39,26,38,27},{63,2,62,3,51,14,50,1..., dimensions={0} | all-to-all | bytes 1048576 | tf_op jit(solution)/shard_map/all_to_all | solution.py:67
  209.8 2.9 gradient.4
  212.7 10.9 %all_to_all.78.in_ref = f32[8,64,256]{2,1,0:T(8,128)S(1)} all-to-all(f32[8,64,256]{2,1,0:T(8,128)S(1)} %gradient.4), channel_id=1, replica_groups={{60,43,63,40,56,47,59,44},{1,22,2,21,5,18,6,17},{61,42,62,41,57,46,58,4..., dimensions={0} | all-to-all | bytes 1048576 | tf_op jit(solution)/shard_map/all_to_all | solution.py:67
  223.7 0.1 collective-permute-start.4
  223.8 1.2 collective-permute-done.4.other_ref
  225.0 0.2 next_step.1
  225.2 12.3 %all_to_all.79.in_ref = f32[8,136,128]{2,1,0:T(8,128)S(1)} all-to-all(f32[8,136,128]{2,1,0:T(8,128)S(1)} %get-tuple-element.99), channel_id=1, replica_groups={{60,43,63,40,56,47,59,44},{1,22,2,21,5,18,6,17},{61,42,62,41,57,46,58,4..., dimensions={0} | all-to-all | bytes 1114112 | tf_op jit(solution)/shard_map/all_to_all | solution.py:67
  237.5 2.7 push.3
  240.3 12.6 %all_to_all.80.in_ref = f32[8,136,128]{2,1,0:T(8,128)S(1)} all-to-all(f32[8,136,128]{2,1,0:T(8,128)S(1)} %push.3), channel_id=1, replica_groups={{60,1,61,0,48,13,49,12},{43,22,42,23,39,26,38,27},{63,2,62,3,51,14,50,1..., dimensions={0} | all-to-all | bytes 1114112 | tf_op jit(solution)/shard_map/all_to_all | solution.py:67
  252.9 0.2 last_residual.1
  253.1 13.1 %all_to_all.81.residual_ref = f32[8,128,128]{2,1,0:T(8,128)S(1)} all-to-all(f32[8,128,128]{2,1,0:T(8,128)S(1)} %get-tuple-element.102), channel_id=1, replica_groups={{60,1,61,0,48,13,49,12},{43,22,42,23,39,26,38,27},{63,2,62,3,51,14,50,1..., dimensions={0} | all-to-all | bytes 1048576 | tf_op jit(solution)/shard_map/all_to_all | solution.py:67
  266.2 2.9 gradient.5
  269.1 10.9 %all_to_all.82.in_ref = f32[8,64,256]{2,1,0:T(8,128)S(1)} all-to-all(f32[8,64,256]{2,1,0:T(8,128)S(1)} %gradient.5), channel_id=1, replica_groups={{60,43,63,40,56,47,59,44},{1,22,2,21,5,18,6,17},{61,42,62,41,57,46,58,4..., dimensions={0} | all-to-all | bytes 1048576 | tf_op jit(solution)/shard_map/all_to_all | solution.py:67
  280.1 0.1 collective-permute-start.5
  280.2 1.2 collective-permute-done.5.other_ref
  281.4 0.2 last_gradient.1
  281.6 16.3 %all_to_all.83 = f32[64,1,128]{2,1,0:T(1,128)S(1)} all-to-all(f32[64,1,128]{2,1,0:T(1,128)S(1)} %bitcast.12), channel_id=1, replica_groups={{0,42,1,43,2,40,3,41,4,46,5,47,6,44,7,45,8,34,9,35,10,32,11,33,12,38,13..., dimensions={0} | all-to-all | bytes 65536 | tf_op jit(solution)/shard_map/all_to_all | solution.py:67
  297.9 0.8 close.1
  (8 shorter events, 0.2 us)
Async XLA Ops:
  0.1 103.5 %copy-start = (f32[64,256]{1,0:T(8,128)S(1)}, f32[64,256]{1,0:T(8,128)}, u32[]{:S(2)}) copy-start(f32[64,256]{1,0:T(8,128)} %anchor_ref.5) | copy-start | bytes 196612
  103.6 5.5 %collective-permute-start = (f32[1,64,256]{2,1,0:T(8,128)S(1)}, f32[1,64,256]{2,1,0:T(8,128)S(1)}, u32[]{:S(2)}, u32[]{:S(2)}) collective-permute-start(f32[1,64,256]{2,1,0:T(8,128)S(1)} %bitcast.9), channel_id=1, source_target_pairs={{60,63},{43,40},{63,60},{40,43},{56,59},{47,44},{59,56},{44,47},{1... | collective-permute-start | bytes 196616 | tf_op jit(solution)/shard_map/ppermute | solution.py:431
  109.0 5.0 %collective-permute-start.1 = (f32[2,64,256]{2,1,0:T(8,128)S(1)}, f32[2,64,256]{2,1,0:T(8,128)S(1)}, u32[]{:S(2)}, u32[]{:S(2)}) collective-permute-start(f32[2,64,256]{2,1,0:T(8,128)S(1)} %beside.3.own_ref), channel_id=1, source_target_pairs={{60,56},{43,47},{63,59},{40,44},{56,60},{47,43},{59,63},{44,40},{1... | collective-permute-start | bytes 393224 | tf_op jit(solution)/shard_map/ppermute | solution.py:431
  114.1 7.6 %collective-permute-start.2 = (f32[4,64,256]{2,1,0:T(8,128)S(1)}, f32[4,64,256]{2,1,0:T(8,128)S(1)}, u32[]{:S(2)}, u32[]{:S(2)}) collective-permute-start(f32[4,64,256]{2,1,0:T(8,128)S(1)} %beside.4.own_ref), channel_id=1, source_target_pairs={{60,44},{43,59},{63,47},{40,56},{56,40},{47,63},{59,43},{44,60},{1... | collective-permute-start | bytes 786440 | tf_op jit(solution)/shard_map/ppermute | solution.py:431
  153.3 15.3 %copy-start.1 = (f32[256]{0:T(256)S(1)}, f32[256]{0:T(256)}, u32[]{:S(2)}) copy-start(f32[256]{0:T(256)} %param.7) | copy-start | bytes 3076
  167.3 1.3 collective-permute-start.3
  223.7 1.3 collective-permute-start.4
  280.1 1.3 collective-permute-start.5
